TPU v7x, 256 devices: a whole 4x4x8 slice. The times are simulated.
256 devices in a mesh: worker: 16 (over z_hi, x), tok: 16 (over z_lo, y, core).
Axes of the slice: x: 4, y: 4, z: 8 (z_hi: 4, z_lo: 2; z = z_hi * 2 + z_lo), core: 2. Of those that a mesh axis runs over, the one named last changes fastest.
Arguments:
- inputs: bfloat16 [16, 24576, 2048], P('worker', 'tok'), may hold values from -6 to 6
- cotangent: bfloat16 [16, 24576, 1024], P('worker', 'tok'), may hold values from -0.038085938 to 0.038085938
- weights: float32 [16, 2048, 1024], P('worker', 'tok'), may hold values from -12 to 12
- momentum: float32 [16, 2048, 1024], P('worker', 'tok'), may hold values from -6 to 6
- mix_weights: int32 [16, 5], P('worker'), may hold values from 1 to 5
- clip_radius: int32 [2], replicated, may hold values from 700 to 2299
Outputs:
- new_weights: float32 [16, 2048, 1024], P('worker', 'tok')
- new_momentum: float32 [16, 2048, 1024], P('worker', 'tok')
All inputs are finite; a program needn't handle non-finite values.
Results may differ from a plain program's by a relative error of at most 0.0003.
Values sent between devices are 32-bit elements; how exact they have to be, the bound alone decides.
A program may use at most 64 MiB of HBM per device.

v0:
```python
import math

import jax
import jax.numpy as jnp
from jax import lax
from jax.sharding import PartitionSpec as P

D = 2048
KV_WIDTH = 512
ROUNDS = 2


LEARNING_RATE = 0.25


def partner(value, axis, apart):
    mask = 2**apart
    pairs = [(source, source ^ mask) for source in range(lax.axis_size(axis))]
    return lax.ppermute(value, axis, pairs)


def shifted(block, axis, distance):
    devices = range(lax.axis_size(axis))
    route = [((i - distance) % len(devices), i) for i in devices]
    return lax.ppermute(block, axis, route)


def copy_for_each(shard, axis):
    copies = jnp.broadcast_to(shard, (lax.axis_size(axis), *shard.shape))
    return lax.all_to_all(copies, axis, split_axis=0, concat_axis=0, tiled=True)


def over_copies(shard, axis):
    return copy_for_each(shard, axis).sum(axis=0)


def gradient_rows(features, columns):
    return lax.dot_general(
        features, columns, (((0,), (0,)), ((), ())), preferred_element_type=jnp.float32
    )


def per_device(inputs, cotangent, weights, momentum, mix_weights, clip_radius):
    features = inputs[0]
    upstream = cotangent[0]
    current = weights[0]
    previous = momentum[0]
    half_width = upstream.shape[1] // 2
    local_rows = current.shape[0]
    gradient = lax.psum_scatter(
        gradient_rows(features, upstream), "tok", scatter_dimension=0, tiled=True
    )
    velocity = 0.5 * previous + gradient
    current = current - LEARNING_RATE * velocity
    mixing = mix_weights[0].astype(jnp.float32)
    shares = mixing / jnp.sum(mixing)
    radius_all = clip_radius.astype(jnp.float32) * (math.sqrt(D * KV_WIDTH) / 1000.0)
    for round_index in range(ROUNDS):
        radius = radius_all[round_index]
        neighbours = (
            partner(current, "worker", 0),
            partner(current, "worker", 1),
            shifted(current, "worker", 4),
            shifted(current, "worker", -4),
        )
        halves_list = [
            (neighbour - current).reshape(local_rows, 2, half_width) for neighbour in neighbours
        ]
        squares = jnp.stack([jnp.sum(halves * halves, axis=(0, 2)) for halves in halves_list])
        totals = over_copies(squares, "tok")
        distance_rows = [totals[position] for position in range(4)]
        mixed_step = jnp.zeros((local_rows, 2, half_width), jnp.float32)
        for position in range(4):
            factor = radius / jnp.maximum(jnp.sqrt(distance_rows[position]), radius)
            mixed_step = (
                mixed_step + halves_list[position] * (shares[position + 1] * factor)[None, :, None]
            )
        current = current + mixed_step.reshape(current.shape)
    return (current[None], velocity[None])


def solution(mesh):
    placed = (
        P("worker", "tok", None),
        P("worker", "tok", None),
        P("worker", "tok", None),
        P("worker", "tok", None),
        P("worker", None),
        P(),
    )
    return jax.shard_map(
        per_device,
        mesh=mesh,
        in_specs=placed,
        out_specs=(P("worker", "tok", None), P("worker", "tok", None)),
        check_vma=False,
    )
```

profile of v0, /device:TPU:8, one launch (start us, length us, event | category | flops | bytes accessed | tf_op | source)
XLA Modules:
  0.0 205.0 jit_solution(6625501219371789676)
XLA Ops:
  7.2 0.0 copy-start
  7.2 0.0 reduce-scatter.2.cloned.1.call-start
  7.2 1.8 copy-done
  9.1 10.8 %fusion = f32[2048,1024]{1,0:T(8,128)} fusion(bf16[1,1536,2048]{2,1,0:T(8,128)(2,1)} %param.6, bf16[1,1536,1024]{2,1,0:T(8,128)(2,1)S(1)} %copy-done), kind=kOutput, calls=%fused_computation | convolution fusion | flops 6442450944 | bytes 17825792 | tf_op jit(solution)/shard_map/dot_general | solution.py:38
  19.9 0.0 copy-start.3
  19.9 0.0 copy-start.4
  19.9 0.0 reduce-scatter.2.cloned.1.call-update
  19.9 0.6 copy-done.3
  20.5 0.6 convert_reduce_fusion
  21.2 74.8 %reduce-scatter.2.cloned.1.call-done = f32[128,1024]{1,0:T(8,128)} async-done(((f32[2048,1024]{1,0:T(8,128)}), f32[128,1024]{1,0:T(8,128)}) %reduce-scatter.2.cloned.1.call-update) | async-done | bytes 524304 | tf_op jit(solution)/shard_map/reduce_scatter | solution.py:50
  96.0 2.3 %fusion.3 = (f32[1,128,1024]{2,1,0:T(8,128)}, f32[128,1024]{1,0:T(8,128)S(1)}) fusion(f32[128,1024]{1,0:T(8,128)} %reduce-scatter.2.cloned.1.call-done, f32[1,128,1024]{2,1,0:T(8,128)} %param.9, f32[1,128,1024]{2,1,0:T(8,128)} %param.8), kind=kLoop, calls=%fused_computation.15 | loop fusion | flops 524288 | bytes 2621440 | tf_op jit(solution)/shard_map/broadcast_in_dim | solution.py:79
  98.2 0.0 copy-start.1
  98.2 1.5 collective-permute-start
  99.7 2.7 %collective-permute-start.1 = (f32[128,1024]{1,0:T(8,128)S(1)}, f32[128,1024]{1,0:T(8,128)S(1)}, u32[]{:S(2)}, u32[]{:S(2)}) collective-permute-start(f32[128,1024]{1,0:T(8,128)S(1)} %get-tuple-element.27), channel_id=1, source_target_pairs={{0,32},{16,48},{32,0},{48,16},{64,96},{80,112},{96,64},{112,80},{1... | collective-permute-start | bytes 1572872 | tf_op jit(solution)/shard_map/ppermute | solution.py:19
  102.4 2.5 %collective-permute-start.2 = (f32[128,1024]{1,0:T(8,128)S(1)}, f32[128,1024]{1,0:T(8,128)S(1)}, u32[]{:S(2)}, u32[]{:S(2)}) collective-permute-start(f32[128,1024]{1,0:T(8,128)S(1)} %get-tuple-element.27), channel_id=1, source_target_pairs={{192,0},{208,16},{224,32},{240,48},{0,64},{16,80},{32,96},{48,112}... | collective-permute-start | bytes 1572872 | tf_op jit(solution)/shard_map/ppermute | solution.py:25
  104.9 1.6 collective-permute-start.3
  106.5 0.6 convert_divide_fusion
  107.1 0.6 fusion.5
  107.8 0.0 copy-done.4
  107.8 5.3 %collective-permute-done = f32[128,1024]{1,0:T(8,128)S(1)} collective-permute-done((f32[128,1024]{1,0:T(8,128)S(1)}, f32[128,1024]{1,0:T(8,128)S(1)}, u32[]{:S(2)}, u32[]{:S(2)}) %collective-permute-start) | collective-permute-done | bytes 524320 | tf_op jit(solution)/shard_map/ppermute | solution.py:19
  113.1 8.3 %collective-permute-done.1 = f32[128,1024]{1,0:T(8,128)S(1)} collective-permute-done((f32[128,1024]{1,0:T(8,128)S(1)}, f32[128,1024]{1,0:T(8,128)S(1)}, u32[]{:S(2)}, u32[]{:S(2)}) %collective-permute-start.1) | collective-permute-done | bytes 524320 | tf_op jit(solution)/shard_map/ppermute | solution.py:19
  121.4 0.0 collective-permute-done.2
  121.4 5.2 %collective-permute-done.3 = f32[128,1024]{1,0:T(8,128)S(1)} collective-permute-done((f32[128,1024]{1,0:T(8,128)S(1)}, f32[128,1024]{1,0:T(8,128)S(1)}, u32[]{:S(2)}, u32[]{:S(2)}) %collective-permute-start.3) | collective-permute-done | bytes 524320 | tf_op jit(solution)/shard_map/ppermute | solution.py:25
  126.6 0.0 copy-done.1
  126.6 1.5 multiply_reduce_fusion.7
  128.2 0.1 reduce_sum.125
  128.3 0.1 reduce_sum.128
  128.4 0.1 reduce_sum.134
  128.6 0.1 reduce_sum.140
  128.7 0.1 copy.14
  128.8 0.6 broadcast_in_dim.8
  129.4 10.1 %all-to-all-start = ((f32[16,4,2]{1,2,0:T(2,128)}), f32[16,4,2]{1,2,0:T(2,128)S(1)}, u32[]{:S(2)}, u32[]{:S(2)}) async-start(f32[16,4,2]{1,2,0:T(2,128)} %broadcast_in_dim.8), calls=%async_computation.1 | async-start | bytes 32768 | tf_op jit(solution)/shard_map/all_to_all | solution.py:30
  139.5 0.6 fusion.4
  140.1 4.1 %all-to-all-done = f32[16,4,2]{1,2,0:T(2,128)S(1)} async-done(((f32[16,4,2]{1,2,0:T(2,128)}), f32[16,4,2]{1,2,0:T(2,128)S(1)}, u32[]{:S(2)}, u32[]{:S(2)}) %all-to-all-start) | async-done | bytes 544 | tf_op jit(solution)/shard_map/all_to_all | solution.py:30
  144.2 3.2 %multiply_reduce_fusion.15 = (f32[2]{0:T(128)S(1)}, f32[2]{0:T(128)S(1)}, f32[2]{0:T(128)S(1)}, f32[2]{0:T(128)S(1)}) fusion(f32[4,2]{0,1:T(2,128)S(1)} %reduce_sum.168, f32[]{:T(128)} %bitcast.5, f32[]{:T(128)} %bitcast.4, f32[]{:T(128)} %bitcast.12, f32[]{:T(128)} %bitcast.11, f32[]{:T(128)} %bitcast.10), kind=kLoop, calls=%fused_computation.33 | loop fusion | flops 24 | bytes 84 | tf_op jit(solution)/shard_map/mul | solution.py:76
  147.4 0.1 broadcast_bitcast_fusion.6
  147.5 0.1 broadcast_bitcast_fusion.4
  147.6 1.9 add_add_fusion
  149.5 0.0 copy-start.2
  149.5 0.3 collective-permute-start.4
  149.8 1.8 collective-permute-start.5
  151.7 4.3 %collective-permute-start.6 = (f32[128,1024]{1,0:T(8,128)S(1)}, f32[128,1024]{1,0:T(8,128)S(1)}, u32[]{:S(2)}, u32[]{:S(2)}) collective-permute-start(f32[128,1024]{1,0:T(8,128)S(1)} %add_add_fusion), channel_id=1, source_target_pairs={{192,0},{208,16},{224,32},{240,48},{0,64},{16,80},{32,96},{48,112}... | collective-permute-start | bytes 1572872 | tf_op jit(solution)/shard_map/ppermute | solution.py:25
  156.0 0.0 collective-permute-start.7
  156.0 8.4 %collective-permute-done.4 = f32[128,1024]{1,0:T(8,128)S(1)} collective-permute-done((f32[128,1024]{1,0:T(8,128)S(1)}, f32[128,1024]{1,0:T(8,128)S(1)}, u32[]{:S(2)}, u32[]{:S(2)}) %collective-permute-start.4) | collective-permute-done | bytes 524320 | tf_op jit(solution)/shard_map/ppermute | solution.py:19
  164.4 10.5 %collective-permute-done.5 = f32[128,1024]{1,0:T(8,128)S(1)} collective-permute-done((f32[128,1024]{1,0:T(8,128)S(1)}, f32[128,1024]{1,0:T(8,128)S(1)}, u32[]{:S(2)}, u32[]{:S(2)}) %collective-permute-start.5) | collective-permute-done | bytes 524320 | tf_op jit(solution)/shard_map/ppermute | solution.py:19
  174.8 2.6 %collective-permute-done.6 = f32[128,1024]{1,0:T(8,128)S(1)} collective-permute-done((f32[128,1024]{1,0:T(8,128)S(1)}, f32[128,1024]{1,0:T(8,128)S(1)}, u32[]{:S(2)}, u32[]{:S(2)}) %collective-permute-start.6) | collective-permute-done | bytes 524320 | tf_op jit(solution)/shard_map/ppermute | solution.py:25
  177.4 2.9 %collective-permute-done.7 = f32[128,1024]{1,0:T(8,128)S(1)} collective-permute-done((f32[128,1024]{1,0:T(8,128)S(1)}, f32[128,1024]{1,0:T(8,128)S(1)}, u32[]{:S(2)}, u32[]{:S(2)}) %collective-permute-start.7) | collective-permute-done | bytes 524320 | tf_op jit(solution)/shard_map/ppermute | solution.py:25
  180.3 0.0 copy-done.2
  180.3 1.5 multiply_reduce_fusion.3
  181.9 0.1 reduce_sum.171
  182.0 0.1 reduce_sum.174
  182.2 0.1 reduce_sum.177
  182.3 0.1 reduce_sum.180
  182.4 0.1 copy.15
  182.5 9.3 %all_to_all.10 = f32[16,4,2]{1,2,0:T(2,128)S(1)} all-to-all(f32[16,4,2]{1,2,0:T(2,128)S(1)} %broadcast_in_dim.9), channel_id=1, replica_groups=mesh['worker'=16,'tok'=16] {'tok'}, dimensions={0} | all-to-all | bytes 1024 | tf_op jit(solution)/shard_map/all_to_all | solution.py:30
  191.9 3.2 %multiply_reduce_fusion.11 = (f32[2]{0:T(128)S(1)}, f32[2]{0:T(128)S(1)}, f32[2]{0:T(128)S(1)}, f32[2]{0:T(128)S(1)}) fusion(f32[4,2]{0,1:T(2,128)S(1)} %reduce_sum.181, f32[]{:T(128)} %bitcast.13, f32[]{:T(128)} %bitcast.4, f32[]{:T(128)} %bitcast.12, f32[]{:T(128)} %bitcast.11, f32[]{:T(128)} %bitcast.10), kind=kLoop, calls=%fused_computation.29 | loop fusion | flops 24 | bytes 84 | tf_op jit(solution)/shard_map/mul | solution.py:76
  195.1 0.1 broadcast_bitcast_fusion.3
  195.2 0.1 broadcast_bitcast_fusion.2
  195.3 0.1 broadcast_bitcast_fusion.1
  195.4 0.1 broadcast_bitcast_fusion
  195.4 2.7 %add_bitcast_fusion = f32[1,128,1024]{2,1,0:T(8,128)} fusion(f32[128,1024]{1,0:T(8,128)} %copy-done.2, f32[128,1024]{1,0:T(8,128)} %get-tuple-element.29, f32[128,1024]{1,0:T(8,128)} %get-tuple-element.31, f32[128,1024]{1,0:T(8,128)} %get-tuple-element.33, f32[128,1024]{1,0:T(8,128)} %get-tuple-element.11, f32[1024]{0:T(1024)S(1)} %bitcast.63, ...), kind=kLoop, calls=%fused_computation.5 | loop fusion | flops 1048576 | bytes 3162112 | tf_op jit(solution)/shard_map/broadcast_in_dim | solution.py:79
  (22 shorter events, 0.2 us)
Async XLA Ops:
  7.2 1.9 copy-start
  7.2 88.8 %reduce-scatter.2.cloned.1.call-start = ((), (), s32[]{:S(2)}) async-start(), calls=%async_computation.3 | async-start | bytes 8912896 | tf_op jit(solution)/shard_map/reduce_scatter | solution.py:50
  19.9 0.7 copy-start.3
  19.9 87.9 %copy-start.4 = (s32[2]{0:T(128)S(1)}, s32[2]{0:T(128)}, u32[]{:S(2)}) copy-start(s32[2]{0:T(128)} %param.11) | copy-start | bytes 28
  98.2 28.4 %copy-start.1 = (f32[128,1024]{1,0:T(8,128)}, f32[128,1024]{1,0:T(8,128)S(1)}, u32[]{:S(2)}) copy-start(f32[128,1024]{1,0:T(8,128)S(1)} %get-tuple-element.27) | copy-start | bytes 1572868
  98.2 14.9 %collective-permute-start = (f32[128,1024]{1,0:T(8,128)S(1)}, f32[128,1024]{1,0:T(8,128)S(1)}, u32[]{:S(2)}, u32[]{:S(2)}) collective-permute-start(f32[128,1024]{1,0:T(8,128)S(1)} %get-tuple-element.27), channel_id=1, source_target_pairs={{0,16},{16,0},{32,48},{48,32},{64,80},{80,64},{96,112},{112,96},{1... | collective-permute-start | bytes 1572872 | tf_op jit(solution)/shard_map/ppermute | solution.py:19
  99.7 21.7 %collective-permute-start.1 = (f32[128,1024]{1,0:T(8,128)S(1)}, f32[128,1024]{1,0:T(8,128)S(1)}, u32[]{:S(2)}, u32[]{:S(2)}) collective-permute-start(f32[128,1024]{1,0:T(8,128)S(1)} %get-tuple-element.27), channel_id=1, source_target_pairs={{0,32},{16,48},{32,0},{48,16},{64,96},{80,112},{96,64},{112,80},{1... | collective-permute-start | bytes 1572872 | tf_op jit(solution)/shard_map/ppermute | solution.py:19
  102.4 19.0 %collective-permute-start.2 = (f32[128,1024]{1,0:T(8,128)S(1)}, f32[128,1024]{1,0:T(8,128)S(1)}, u32[]{:S(2)}, u32[]{:S(2)}) collective-permute-start(f32[128,1024]{1,0:T(8,128)S(1)} %get-tuple-element.27), channel_id=1, source_target_pairs={{192,0},{208,16},{224,32},{240,48},{0,64},{16,80},{32,96},{48,112}... | collective-permute-start | bytes 1572872 | tf_op jit(solution)/shard_map/ppermute | solution.py:25
  104.9 21.7 %collective-permute-start.3 = (f32[128,1024]{1,0:T(8,128)S(1)}, f32[128,1024]{1,0:T(8,128)S(1)}, u32[]{:S(2)}, u32[]{:S(2)}) collective-permute-start(f32[128,1024]{1,0:T(8,128)S(1)} %get-tuple-element.27), channel_id=1, source_target_pairs={{64,0},{80,16},{96,32},{112,48},{128,64},{144,80},{160,96},{176,11... | collective-permute-start | bytes 1572872 | tf_op jit(solution)/shard_map/ppermute | solution.py:25
  129.4 14.8 %all-to-all-start = ((f32[16,4,2]{1,2,0:T(2,128)}), f32[16,4,2]{1,2,0:T(2,128)S(1)}, u32[]{:S(2)}, u32[]{:S(2)}) async-start(f32[16,4,2]{1,2,0:T(2,128)} %broadcast_in_dim.8), calls=%async_computation.1 | async-start | bytes 32768 | tf_op jit(solution)/shard_map/all_to_all | solution.py:30
  149.5 30.8 %copy-start.2 = (f32[128,1024]{1,0:T(8,128)}, f32[128,1024]{1,0:T(8,128)S(1)}, u32[]{:S(2)}) copy-start(f32[128,1024]{1,0:T(8,128)S(1)} %add_add_fusion) | copy-start | bytes 1572868
  149.5 14.9 %collective-permute-start.4 = (f32[128,1024]{1,0:T(8,128)S(1)}, f32[128,1024]{1,0:T(8,128)S(1)}, u32[]{:S(2)}, u32[]{:S(2)}) collective-permute-start(f32[128,1024]{1,0:T(8,128)S(1)} %add_add_fusion), channel_id=1, source_target_pairs={{0,16},{16,0},{32,48},{48,32},{64,80},{80,64},{96,112},{112,96},{1... | collective-permute-start | bytes 1572872 | tf_op jit(solution)/shard_map/ppermute | solution.py:19
  149.8 25.0 %collective-permute-start.5 = (f32[128,1024]{1,0:T(8,128)S(1)}, f32[128,1024]{1,0:T(8,128)S(1)}, u32[]{:S(2)}, u32[]{:S(2)}) collective-permute-start(f32[128,1024]{1,0:T(8,128)S(1)} %add_add_fusion), channel_id=1, source_target_pairs={{0,32},{16,48},{32,0},{48,16},{64,96},{80,112},{96,64},{112,80},{1... | collective-permute-start | bytes 1572872 | tf_op jit(solution)/shard_map/ppermute | solution.py:19
  151.7 25.8 %collective-permute-start.6 = (f32[128,1024]{1,0:T(8,128)S(1)}, f32[128,1024]{1,0:T(8,128)S(1)}, u32[]{:S(2)}, u32[]{:S(2)}) collective-permute-start(f32[128,1024]{1,0:T(8,128)S(1)} %add_add_fusion), channel_id=1, source_target_pairs={{192,0},{208,16},{224,32},{240,48},{0,64},{16,80},{32,96},{48,112}... | collective-permute-start | bytes 1572872 | tf_op jit(solution)/shard_map/ppermute | solution.py:25
  156.0 24.3 %collective-permute-start.7 = (f32[128,1024]{1,0:T(8,128)S(1)}, f32[128,1024]{1,0:T(8,128)S(1)}, u32[]{:S(2)}, u32[]{:S(2)}) collective-permute-start(f32[128,1024]{1,0:T(8,128)S(1)} %add_add_fusion), channel_id=1, source_target_pairs={{64,0},{80,16},{96,32},{112,48},{128,64},{144,80},{160,96},{176,11... | collective-permute-start | bytes 1572872 | tf_op jit(solution)/shard_map/ppermute | solution.py:25
Sparse Core Ops, SparseCore 0:
  20.0 75.8 reduce-scatter.1
where the time goes:
time: 208 us; the launch traced here: 205 us
  waiting for transfers between devices  122 us (59%)
  starting transfers between devices  24.9 us (12%)
  other arithmetic  18.8 us (9%)
  between operations  14.1 us (7%)
  matrix products  10.8 us (5%)
  blocking collectives  9.34 us (4%)
  local copies, waits for them, and re-layouts  5.04 us (2%)
    reduce_scatter x1, waiting for transfers between devices, per_device(): lax.psum_scatter(gradient_rows(features, upstream), 'tok', scatter_dimens...  74.8 us
    ppermute x4, waiting for transfers between devices, partner(): return lax.ppermute(value, axis, pairs)  32.4 us
    dot_general x1, matrix products, gradient_rows(): lax.dot_general(features, columns, (((0,), (0,)), ((), ())), preferred_el...  10.8 us
    ppermute x4, waiting for transfers between devices, shifted(): return lax.ppermute(block, axis, route)  10.7 us
    all_to_all x1, starting transfers between devices, copy_for_each(): return lax.all_to_all(copies, axis, split_axis=0, concat_axis=0, tiled=True)  10.1 us
    all_to_all x1, blocking collectives, copy_for_each(): return lax.all_to_all(copies, axis, split_axis=0, concat_axis=0, tiled=True)  9.34 us
    ppermute x4, starting transfers between devices, shifted(): return lax.ppermute(block, axis, route)  8.44 us
    mul x2, other arithmetic, per_device(): shares[position + 1] * factor  6.41 us
  transfers between devices with their start and end apart: 10, of which 9 were waited for; matrix products, arithmetic and copies ran while one was open for 1% of the time, Pallas kernels for 0%

commit v1 on v0

v1 whole, which is shorter than its diff:
```python
import math

import jax
import jax.numpy as jnp
from jax import lax
from jax.experimental import pallas as pl
from jax.experimental.pallas import tpu as pltpu
from jax.sharding import PartitionSpec as P

D = 2048
KV_WIDTH = 512
ROUNDS = 2
LEARNING_RATE = 0.25

MESH = pl.DeviceIdType.MESH
F32 = jnp.float32
BF16 = jnp.bfloat16
HIGHEST = lax.Precision.HIGHEST

ORDER = ((1, 2), (0, 2), (1, 1), (1, 3), (1, 0), (0, 1), (0, 3), (0, 0))
PAIRS = 3


def kernel(
    feat, cot, wts, mom, mix, clip, o_new, o_vel,
    F, C, PA, PR, Y1, Y2, ZR, ZF, W1, W2, WT, MO, CUR, RX, NEW, NR, DP, PAY, R1, R2, MS, MR, KC,
    ld, d_s, d_r, y1_s, y1_r, y2_s, y2_r, z_s, z_r, zf_s, zf_r, w1_s, w1_r, w2_s, w2_r,
    a_s, a_r, m_s, m_r, r_s, r_r, b_s, b_r,
):
    t = lax.axis_index("tok")
    w = lax.axis_index("worker")
    q, y, c = t // 8, (t // 2) % 4, t % 2
    flip = (1 - q) * 8 + y * 2 + c
    sibling = {"worker": w, "tok": q * 8 + y * 2 + (1 - c)}
    up = {"worker": w, "tok": q * 8 + lax.rem(y + 1, 4) * 2 + c}
    down = {"worker": w, "tok": q * 8 + lax.rem(y + 3, 4) * 2 + c}
    across = {"worker": w, "tok": flip}
    tok_peers = [{"worker": w, "tok": lax.rem(t + i, 16)} for i in range(1, 16)]
    work_peers = [{"worker": lax.rem(w + i, 16), "tok": flip} for i in range(1, 16)]

    barrier = pltpu.get_barrier_semaphore()
    for peer in tok_peers + work_peers:
        pl.semaphore_signal(barrier, inc=1, device_id=peer, device_id_type=MESH)

    def load(src, dst, i):
        cp = pltpu.make_async_copy(src, dst, ld.at[i])
        cp.start()
        return cp

    def send(src, dst, ss, rs, peer):
        cp = pltpu.make_async_remote_copy(
            src_ref=src, dst_ref=dst, send_sem=ss, recv_sem=rs, device_id=peer, device_id_type=MESH
        )
        cp.start()
        return cp

    def wait_bytes(ref, sem):
        pltpu.make_async_copy(ref, ref, sem).wait()

    def feat_block(j):
        dq, dy = ORDER[j]
        chip = (q + dq) % 2 * 4 + lax.rem(y + dy, 4)
        return feat.at[:, pl.ds(pl.multiple_of(chip * 256, 256), 256)]

    f_loads = [load(feat_block(0), F.at[0], 0)]
    c_loads = [load(cot.at[:, n * 256 : (n + 1) * 256], C.at[n], 8 + n) for n in range(4)]
    f_loads += [load(feat_block(j), F.at[j], j) for j in range(1, 8)]
    w_load, m_load = load(wts, WT, 12), load(mom, MO, 13)

    MS[...] = jnp.zeros_like(MS)
    MS[0:1, 0:5] = mix[...].astype(F32)
    MR[w] = MS[...]
    for half in range(2):
        for i in range(16):
            DP[half * 256 + i * 17 : half * 256 + i * 17 + 1, :] = jnp.zeros((1, 128), F32)

    sends = []

    def multiply(j):
        dq, dy = ORDER[j]
        f_loads[j].wait()
        if j == 0:
            for cp in c_loads:
                cp.wait()

        def columns(n, _):
            r = lax.dot_general(F[j], C[n], (((0,), (0,)), ((), ())), preferred_element_type=F32)
            for core in range(2):
                for k in range(2):
                    PA[core, dq, dy, 2 * n + k] = r[core * 128 : core * 128 + 128, k * 128 : k * 128 + 128]
            return 0

        lax.fori_loop(0, 4, columns, 0)

    mine = PA.at[c]

    def to_sibling(j):
        dq, dy = ORDER[j]
        return send(PA.at[1 - c, dq, dy], PR.at[dq, dy], d_s.at[j], d_r.at[j], sibling)

    def add_sibling(j, cp):
        dq, dy = ORDER[j]
        cp.wait_recv()
        mine[dq, dy] = mine[dq, dy] + PR[dq, dy]

    multiply(0)
    pl.semaphore_wait(barrier, 30)
    d = [to_sibling(0)]
    for peer in work_peers:
        send(MS, MR.at[w], m_s.at[0], m_r.at[0], peer)

    zf, y1 = {}, {}

    def first_across(dy):
        zf[dy] = send(mine.at[1, dy, 6:8], ZF.at[dy], zf_s.at[dy], zf_r.at[dy], across)

    for j in range(1, 8):
        multiply(j)
        d.append(to_sibling(j))
        add_sibling(j - 1, d[j - 1])
        if j == 2:
            for k in range(6):
                y1[k] = send(mine.at[:, 2, k], Y1.at[k], y1_s.at[k], y1_r.at[k], (up, down)[k % 2])
            first_across(2)
        if 3 <= j <= 5:
            first_across(ORDER[j - 1][1])
    add_sibling(7, d[7])

    y2 = {}

    def second(p):
        a, b = 2 * p, 2 * p + 1
        y1[a].wait_recv()
        mine[:, 1, a] = mine[:, 1, a] + Y1[a]
        y2[0, a] = send(mine.at[:, 1, a], Y2.at[0, a], y2_s.at[0, a], y2_r.at[0, a], up)
        y1[b].wait_recv()
        mine[:, 3, b] = mine[:, 3, b] + Y1[b]
        y2[1, b] = send(mine.at[:, 3, b], Y2.at[1, b], y2_s.at[1, b], y2_r.at[1, b], down)
        y2[0, b] = send(mine.at[:, 1, b], Y2.at[0, b], y2_s.at[0, b], y2_r.at[0, b], up)
        y2[1, a] = send(mine.at[:, 3, a], Y2.at[1, a], y2_s.at[1, a], y2_r.at[1, a], down)

    z = {}

    def own(p):
        for k in (2 * p, 2 * p + 1):
            y2[0, k].wait_recv()
            y2[1, k].wait_recv()
            mine[:, 0, k] = mine[:, 0, k] + Y2[0, k] + Y2[1, k]
        z[p] = send(mine.at[1, 0, 2 * p : 2 * p + 2], ZR.at[p], z_s.at[p], z_r.at[p], across)

    def step(k, gradient):
        cols = slice(k * 128, k * 128 + 128)
        velocity = 0.5 * MO[:, cols] + gradient
        o_vel[:, cols] = velocity
        CUR[:, cols] = WT[:, cols] - LEARNING_RATE * velocity

    def transpose_out(p):
        cols = slice(p * 256, p * 256 + 256)
        for i in range(16):
            to = lax.rem(w + i, 16)
            rows = pl.ds(pl.multiple_of(to * 8, 8), 8)
            send(CUR.at[rows, cols], RX.at[w, :, cols], a_s.at[p], a_r.at[p], {"worker": to, "tok": flip})

    def finish(p):
        z[p].wait_recv()
        for k in range(2):
            step(2 * p + k, mine[0, 0, 2 * p + k] + ZR[p, k])
        transpose_out(p)

    w1, w2 = {}, {}

    def across_one():
        for dy in (2, 1, 3, 0):
            zf[dy].wait_recv()
            mine[0, dy, 6:8] = mine[0, dy, 6:8] + ZF[dy]
        for k in range(2):
            w1[k] = send(mine.at[0, 2, 6 + k], W1.at[k], w1_s.at[k], w1_r.at[k], (up, down)[k])

    def across_two():
        for k in range(2):
            dy = (1, 3)[k]
            w1[k].wait_recv()
            mine[0, dy, 6 + k] = mine[0, dy, 6 + k] + W1[k]
        for side in range(2):
            w2[side] = send(
                mine.at[0, (1, 3)[side], 6:8], W2.at[side], w2_s.at[side], w2_r.at[side], (up, down)[side]
            )

    w_load.wait()
    m_load.wait()
    second(0)
    second(1)
    own(0)
    across_one()
    second(2)
    finish(0)
    own(1)
    across_two()
    finish(1)

    def distances(half):
        for bi in range(4):
            for bj in range(bi, 4):
                acc = {}
                for tile in range(4):
                    cols = slice(half * 512 + tile * 128, half * 512 + tile * 128 + 128)
                    left = [RX[4 * bi + i, :, cols] for i in range(4)]
                    right = left if bi == bj else [RX[4 * bj + i, :, cols] for i in range(4)]
                    for i in range(4):
                        for j in range(i + 1 if bi == bj else 0, 4):
                            diff = left[i] - right[j]
                            acc[i, j] = diff * diff if tile == 0 else acc[i, j] + diff * diff
                for (i, j), total in acc.items():
                    row = jnp.sum(total, axis=0, keepdims=True)
                    for a, b in ((4 * bi + i, 4 * bj + j), (4 * bj + j, 4 * bi + i)):
                        at = half * 256 + a * 16 + b
                        DP[at : at + 1, :] = row

    def wait_rows(p):
        wait_bytes(RX.at[:, :, p * 256 : p * 256 + 256], a_r.at[p])

    own(2)
    wait_rows(0)
    wait_rows(1)
    distances(0)
    finish(2)
    for side in range(2):
        w2[side].wait_recv()
    for k in range(2):
        step(6 + k, mine[0, 0, 6 + k] + W2[0, k] + W2[1, k])
    transpose_out(3)

    wait_bytes(MR.at[0:15], m_r.at[0])
    wait_rows(2)
    wait_rows(3)
    distances(1)

    packed = lax.dot_general(
        jnp.ones((8, 128), F32), DP[...], (((1,), (1,)), ((), ())), precision=HIGHEST, preferred_element_type=F32
    )
    PAY[0] = jnp.zeros((8, 128), F32)
    for r in range(4):
        PAY[0, r : r + 1, :] = packed[0:1, r * 128 : r * 128 + 128]
    for stage, (peers, got) in enumerate(((tok_peers, R1), (work_peers, R2))):
        for i, peer in enumerate(peers):
            send(PAY.at[stage, 0:4], got.at[i, 0:4], r_s.at[stage], r_r.at[stage], peer)
        total = PAY[stage, 0:4]
        wait_bytes(got.at[:, 0:4], r_r.at[stage])
        for i in range(15):
            total = total + got[i, 0:4]
        PAY[stage + 1, 0:4] = total

    row = lax.broadcasted_iota(jnp.int32, (32, 128), 0)
    lane = lax.broadcasted_iota(jnp.int32, (32, 128), 1)
    me = row & 15
    base = row - me
    masks = [
        (lane == base + other).astype(F32) for other in (me ^ 1, me ^ 2, (me + 12) & 15, (me + 4) & 15)
    ]
    eye = (lane == row).astype(F32)
    spread = jnp.concatenate([jnp.broadcast_to(PAY[2, r : r + 1, :], (8, 128)) for r in range(4)], axis=0)
    spread = jnp.where((lane >> 4) == (row & 7), spread, 0.0)
    from_lane = lax.broadcasted_iota(jnp.int32, (128, 128), 0)
    to_lane = lax.broadcasted_iota(jnp.int32, (128, 128), 1)
    pick = ((from_lane & 15) == (to_lane & 15)).astype(F32)
    dist2 = jnp.dot(spread, pick, precision=HIGHEST, preferred_element_type=F32)
    dist2 = jnp.where((lane >> 4) == (row >> 4), dist2, 0.0)
    pad = jnp.zeros((96, 128), F32)

    mixing = MR[:, 0, :]
    lane16 = lax.broadcasted_iota(jnp.int32, (16, 128), 1)
    shares = mixing / jnp.sum(mixing, axis=1, keepdims=True)
    share = []
    for k in range(4):
        one = jnp.sum(jnp.where(lane16 == k + 1, shares, 0.0), axis=1, keepdims=True)
        share.append(jnp.concatenate([one, one], axis=0))

    for round_index in range(ROUNDS):
        radius = clip[round_index].astype(F32) * (math.sqrt(D * KV_WIDTH) / 1000.0)
        moves = []
        for k in range(4):
            squares = jnp.sum(dist2 * masks[k], axis=1, keepdims=True)
            factor = radius / jnp.maximum(jnp.sqrt(jnp.maximum(squares, 0.0)), radius)
            moves.append(jnp.broadcast_to(share[k] * factor, (32, 128)))
            KC[round_index, k] = moves[k]
        if round_index == 0:
            mixer = eye * (1.0 - (moves[0] + moves[1] + moves[2] + moves[3]))
            for k in range(4):
                mixer = mixer + masks[k] * moves[k]
            left = jnp.dot(
                mixer, jnp.concatenate([dist2, pad], axis=0), precision=HIGHEST, preferred_element_type=F32
            )
            both = lax.dot_general(
                left, jnp.concatenate([mixer, pad], axis=0), (((1,), (1,)), ((), ())),
                precision=HIGHEST, preferred_element_type=F32,
            )
            diagonal = both * eye
            by_row = jnp.sum(diagonal, axis=1, keepdims=True)
            by_lane = jnp.sum(diagonal, axis=0, keepdims=True)
            dist2 = both - 0.5 * (by_row + by_lane)

    neighbours = [(i ^ 1, i ^ 2, (i - 4) % 16, (i + 4) % 16) for i in range(16)]

    def mixed(round_index, half, blocks):
        out = []
        for i in range(16):
            moved = None
            for k, j in enumerate(neighbours[i]):
                by = jnp.broadcast_to(KC[round_index, k, half * 16 + i : half * 16 + i + 1, :], (8, 128))
                term = by * (blocks[j] - blocks[i])
                moved = term if moved is None else moved + term
            out.append(blocks[i] + moved)
        return out

    here = pl.ds(pl.multiple_of(w * 8, 8), 8)
    for half in range(2):
        for tile in range(4):
            cols = slice(half * 512 + tile * 128, half * 512 + tile * 128 + 128)
            blocks = [RX[i, :, cols] for i in range(16)]
            for round_index in range(ROUNDS):
                blocks = mixed(round_index, half, blocks)
            for i in range(16):
                NEW[i, :, cols] = blocks[i]
        cols = slice(half * 512, half * 512 + 512)
        for i in range(16):
            to = lax.rem(w + i, 16)
            send(NEW.at[to, :, cols], NR.at[here, cols], b_s.at[half], b_r.at[half], {"worker": to, "tok": flip})

    for cp in d + list(y1.values()) + list(y2.values()) + list(z.values()):
        cp.wait_send()
    for cp in list(zf.values()) + list(w1.values()) + list(w2.values()):
        cp.wait_send()
    wait_bytes(MR.at[0:15], m_s.at[0])
    for stage, got in enumerate((R1, R2)):
        wait_bytes(got.at[:, 0:4], r_s.at[stage])
    for p in range(4):
        wait_bytes(CUR.at[:, p * 256 : p * 256 + 256], a_s.at[p])
    for half in range(2):
        cols = slice(half * 512, half * 512 + 512)
        wait_bytes(NR.at[:, cols], b_r.at[half])
        o_new[:, cols] = NR[:, cols]
    for half in range(2):
        wait_bytes(NR.at[:, half * 512 : half * 512 + 512], b_s.at[half])


def per_device(inputs, cotangent, weights, momentum, mix_weights, clip_radius):
    vmem = pl.BlockSpec(memory_space=pltpu.VMEM)
    hbm = pl.BlockSpec(memory_space=pl.ANY)
    dma = pltpu.SemaphoreType.DMA
    block = jax.ShapeDtypeStruct((128, 1024), F32)
    new, velocity = pl.pallas_call(
        kernel,
        out_shape=(block, block),
        in_specs=[hbm, hbm, hbm, hbm, vmem, pl.BlockSpec(memory_space=pltpu.SMEM)],
        out_specs=(vmem, vmem),
        scratch_shapes=[
            pltpu.VMEM((8, 1536, 256), BF16),
            pltpu.VMEM((4, 1536, 256), BF16),
            pltpu.VMEM((2, 2, 4, 8, 128, 128), F32),
            pltpu.VMEM((2, 4, 8, 128, 128), F32),
            pltpu.VMEM((6, 2, 128, 128), F32),
            pltpu.VMEM((2, 6, 2, 128, 128), F32),
            pltpu.VMEM((3, 2, 128, 128), F32),
            pltpu.VMEM((4, 2, 128, 128), F32),
            pltpu.VMEM((2, 128, 128), F32),
            pltpu.VMEM((2, 2, 128, 128), F32),
            pltpu.VMEM((128, 1024), F32),
            pltpu.VMEM((128, 1024), F32),
            pltpu.VMEM((128, 1024), F32),
            pltpu.VMEM((16, 8, 1024), F32),
            pltpu.VMEM((16, 8, 1024), F32),
            pltpu.VMEM((128, 1024), F32),
            pltpu.VMEM((512, 128), F32),
            pltpu.VMEM((3, 8, 128), F32),
            pltpu.VMEM((15, 8, 128), F32),
            pltpu.VMEM((15, 8, 128), F32),
            pltpu.VMEM((8, 128), F32),
            pltpu.VMEM((16, 8, 128), F32),
            pltpu.VMEM((2, 4, 32, 128), F32),
            dma((14,)),
            dma((8,)), dma((8,)),
            dma((6,)), dma((6,)),
            dma((2, 6)), dma((2, 6)),
            dma((3,)), dma((3,)),
            dma((4,)), dma((4,)),
            dma((2,)), dma((2,)),
            dma((2,)), dma((2,)),
            dma((4,)), dma((4,)),
            dma((1,)), dma((1,)),
            dma((2,)), dma((2,)),
            dma((2,)), dma((2,)),
        ],
        compiler_params=pltpu.CompilerParams(
            collective_id=0, has_side_effects=True, vmem_limit_bytes=56 * 1024 * 1024
        ),
    )(inputs[0], cotangent[0], weights[0], momentum[0], mix_weights, clip_radius)
    return (new[None], velocity[None])


def solution(mesh):
    placed = (
        P("worker", "tok", None),
        P("worker", "tok", None),
        P("worker", "tok", None),
        P("worker", "tok", None),
        P("worker", None),
        P(),
    )
    return jax.shard_map(
        per_device,
        mesh=mesh,
        in_specs=placed,
        out_specs=(P("worker", "tok", None), P("worker", "tok", None)),
        check_vma=False,
    )
```

time: 208 us -> 93.1 us (0.45)
  waiting for transfers between devices: 122 us -> 0 us
  Pallas kernels: 0 us -> 86.9 us
  starting transfers between devices: 24.9 us -> 0 us
  other arithmetic: 18.8 us -> 0 us
  between operations: 14.1 us -> 0.64 us
  matrix products: 10.8 us -> 0 us
  blocking collectives: 9.34 us -> 0 us
    pallas_call x0 -> x1, Pallas kernels: none -> 86.9 us  [per_device(): pl.pallas_call(kernel, out_shape=(block, block), in_specs=[hbm, hbm, hbm,...]
    reduce_scatter x1 -> x0, waiting for transfers between devices: 74.8 us -> none  [per_device(): lax.psum_scatter(gradient_rows(features, upstream), 'tok', scatter_dimens...]
    ppermute x8 -> x0, waiting for transfers between devices: 43.1 us -> none  [the longest x4 32.4 us: partner(): return lax.ppermute(value, axis, pairs)]
    ppermute x8 -> x0, starting transfers between devices: 14.7 us -> none  [the longest x4 8.44 us: shifted(): return lax.ppermute(block, axis, route)]
    dot_general x1 -> x0, matrix products: 10.8 us -> none  [gradient_rows(): lax.dot_general(features, columns, (((0,), (0,)), ((), ())), preferred_el...]
    all_to_all x1 -> x0, starting transfers between devices: 10.1 us -> none  [copy_for_each(): return lax.all_to_all(copies, axis, split_axis=0, concat_axis=0, tiled=True)]
    all_to_all x1 -> x0, blocking collectives: 9.34 us -> none  [copy_for_each(): return lax.all_to_all(copies, axis, split_axis=0, concat_axis=0, tiled=True)]
    mul x3 -> x0, other arithmetic: 6.42 us -> none  [the longest x2 6.41 us: per_device(): shares[position + 1] * factor]
  transfers between devices with their start and end apart: 10 -> 0, of which waited for: 9 -> 0; matrix products, arithmetic and copies ran while one was open for 1% -> 0% of each run, Pallas kernels for 0% -> 0%
where the time goes in v1:
time: 93.1 us; the launch traced here: 91.3 us
  Pallas kernels  86.9 us (93%)
  local copies, waits for them, and re-layouts  3.77 us (4%)
    pallas_call x1, Pallas kernels, per_device(): pl.pallas_call(kernel, out_shape=(block, block), in_specs=[hbm, hbm, hbm,...  86.9 us
    unnamed x2, local copies, waits for them, and re-layouts  3.77 us

profile of v1, /device:TPU:8, one launch (start us, length us, event | category | flops | bytes accessed | tf_op | source)
XLA Modules:
  0.0 91.3 jit_solution(16689409591401904405)
XLA Ops:
  0.6 86.9 %shard_map.77 = (f32[128,1024]{1,0:T(8,128)}, f32[128,1024]{1,0:T(8,128)}) custom-call(bf16[1536,2048]{1,0:T(8,128)(2,1)} %bitcast.6, bf16[1536,1024]{1,0:T(8,128)(2,1)} %bitcast.7, f32[128,1024]{1,0:T(8,128)} %bitcast.10, f32[128,1024]{1,0:T(8,128)} %bitcast.11, s32[1,5]{1,0:T(1,128)} %mix.1, s32[2]{0:T(128)} %clip.1), custom_call_target="tpu_custom_call" | custom-call | tf_op jit(solution)/shard_map/pallas_call | solution.py:351
  87.5 1.9 %copy.10 = f32[1,128,1024]{2,1,0:T(8,128)} copy(f32[1,128,1024]{2,1,0:T(8,128)} %bitcast.9) | data formatting | bytes 1048576
  89.4 1.9 %copy.11 = f32[1,128,1024]{2,1,0:T(8,128)} copy(f32[1,128,1024]{2,1,0:T(8,128)} %bitcast.8) | data formatting | bytes 1048576

commit v2 on v1

v2 whole, which is shorter than its diff:
```python
import math

import jax
import jax.numpy as jnp
from jax import lax
from jax.experimental import pallas as pl
from jax.experimental.pallas import tpu as pltpu
from jax.sharding import PartitionSpec as P

D = 2048
KV_WIDTH = 512
ROUNDS = 2
LEARNING_RATE = 0.25

MESH = pl.DeviceIdType.MESH
F32 = jnp.float32
BF16 = jnp.bfloat16
HIGHEST = lax.Precision.HIGHEST

ORDER = ((1, 2), (0, 2), (1, 1), (0, 1), (1, 3), (0, 3), (1, 0), (0, 0))
PAIRS = 3


def kernel(
    feat, cot, wts, mom, mix, clip, o_move, o_grad,
    F, C, PA, PR, Y1, Y2, ZR, ZF, W1, W2, WT, MO, CUR, GR, RX, NEW, DP, PAY, R1, R2, MS, MR, KC,
    ld, d_s, d_r, y1_s, y1_r, y2_s, y2_r, z_s, z_r, zf_s, zf_r, w1_s, w1_r, w2_s, w2_r,
    a_s, a_r, m_s, m_r, r_s, r_r, b_s, b_r, g_s, far,
):
    t = lax.axis_index("tok")
    w = lax.axis_index("worker")
    q, y, c = t // 8, (t // 2) % 4, t % 2
    flip = (1 - q) * 8 + y * 2 + c
    sibling = {"worker": w, "tok": q * 8 + y * 2 + (1 - c)}
    up = {"worker": w, "tok": q * 8 + lax.rem(y + 1, 4) * 2 + c}
    down = {"worker": w, "tok": q * 8 + lax.rem(y + 3, 4) * 2 + c}
    across = {"worker": w, "tok": flip}
    h, x = w // 4, w % 4
    tok_peers = [
        {"worker": w, "tok": (q + dq) % 2 * 8 + lax.rem(y + dy, 4) * 2 + (c + dc) % 2}
        for dy in (2, 1, 3, 0) for dq in (1, 0) for dc in (1, 0)
    ][:-1]
    others = [lax.rem(h + dh, 4) * 4 + lax.rem(x + dx, 4) for dx in (2, 1, 3, 0) for dh in (2, 1, 3, 0)]
    work_peers = [{"worker": other, "tok": flip} for other in others[:-1]]
    beyond = lax.rem(h + 2 * q + 3, 4)
    next_to = [sibling, up, down, across] + [
        {"worker": h * 4 + lax.rem(x + 1, 4), "tok": t},
        {"worker": h * 4 + lax.rem(x + 3, 4), "tok": t},
        {"worker": beyond * 4 + x, "tok": flip},
    ]

    def tell(n):
        for peer in next_to:
            pl.semaphore_signal(far.at[n], inc=1, device_id=peer, device_id_type=MESH)

    def heard(n):
        pl.semaphore_wait(far.at[n], 7)

    barrier = pltpu.get_barrier_semaphore()

    def load(src, dst, i):
        cp = pltpu.make_async_copy(src, dst, ld.at[i])
        cp.start()
        return cp

    def send(src, dst, ss, rs, peer):
        cp = pltpu.make_async_remote_copy(
            src_ref=src, dst_ref=dst, send_sem=ss, recv_sem=rs, device_id=peer, device_id_type=MESH
        )
        cp.start()
        return cp

    def wait_bytes(ref, sem):
        pltpu.make_async_copy(ref, ref, sem).wait()

    def feat_block(j):
        dq, dy = ORDER[j]
        chip = (q + dq) % 2 * 4 + lax.rem(y + dy, 4)
        return feat.at[:, pl.ds(pl.multiple_of(chip * 256, 256), 256)]

    def load_feat(j):
        f_loads[j] = load(feat_block(j), F.at[j], j)

    def load_cot(n):
        c_loads[n] = load(cot.at[:, n * 256 : (n + 1) * 256], C.at[n], 8 + n)

    f_loads, c_loads = {}, {}
    load_feat(0)
    load_cot(0)
    load_feat(1)
    for peer in next_to:
        pl.semaphore_signal(barrier, inc=1, device_id=peer, device_id_type=MESH)

    MS[...] = jnp.zeros_like(MS)
    MS[0:1, 0:5] = mix[...].astype(F32)
    MR[w] = MS[...]
    for half in range(2):
        for i in range(16):
            DP[half * 256 + i * 17 : half * 256 + i * 17 + 1, :] = jnp.zeros((1, 128), F32)

    mine = PA.at[c]

    def product(j, n):
        dq, dy = ORDER[j]
        r = lax.dot_general(F[j], C[n], (((0,), (0,)), ((), ())), preferred_element_type=F32)
        for core in range(2):
            for k in range(2):
                PA[core, dq, dy, 2 * n + k] = r[core * 128 : core * 128 + 128, k * 128 : k * 128 + 128]

    d, zf, y1 = {}, {}, {}

    def first_across(dy):
        zf[dy] = send(mine.at[1, dy, 6:8], ZF.at[dy], zf_s.at[dy], zf_r.at[dy], across)

    def opposite(n):
        d[n].wait_recv()
        for dq in range(2):
            for k in (2 * n, 2 * n + 1):
                mine[dq, 2, k] = mine[dq, 2, k] + PR[dq, 2, k]
        if n < PAIRS:
            for k in (2 * n, 2 * n + 1):
                y1[k] = send(mine.at[:, 2, k], Y1.at[k], y1_s.at[k], y1_r.at[k], (up, down)[k % 2])
        else:
            first_across(2)

    for n in range(4):
        for j in range(2):
            if n == 0:
                f_loads[j].wait()
            if j == 0:
                c_loads[n].wait()
            if n == 0 and j == 0:
                load_cot(1)
                load_cot(2)
            product(j, n)
        if n == 0:
            load_cot(3)
            load_feat(2)
            pl.semaphore_wait(barrier, 7)
        else:
            load_feat(2 * n + 1)
            if n < 3:
                load_feat(2 * n + 2)
        d[n] = send(PA.at[1 - c, :, 2, 2 * n : 2 * n + 2], PR.at[:, 2, 2 * n : 2 * n + 2], d_s.at[n], d_r.at[n], sibling)
        if n >= 1:
            opposite(n - 1)
    w_load, m_load = load(wts, WT, 12), load(mom, MO, 13)
    tell(0)

    def add_sibling(j):
        dq, dy = ORDER[j]
        d[j + 2].wait_recv()
        mine[dq, dy] = mine[dq, dy] + PR[dq, dy]
        if dq == 1:
            first_across(dy)

    y2 = {}

    def along(side, k):
        to, dy = ((up, 1), (down, 3))[side]
        y2[side, k] = send(mine.at[:, dy, k], Y2.at[side, k], y2_s.at[side, k], y2_r.at[side, k], to)

    def plain(k):
        along(1 - k % 2, k)

    def joined(k):
        side, dy = k % 2, (1, 3)[k % 2]
        y1[k].wait_recv()
        mine[:, dy, k] = mine[:, dy, k] + Y1[k]
        along(side, k)

    for j in range(2, 8):
        dq, dy = ORDER[j]
        f_loads[j].wait()
        for n in range(4):
            product(j, n)
        d[j + 2] = send(PA.at[1 - c, dq, dy], PR.at[dq, dy], d_s.at[j + 2], d_r.at[j + 2], sibling)
        if j == 2:
            opposite(3)
        else:
            add_sibling(j - 1)
        if j == 4:
            plain(1)
            heard(0)
            tell(1)
        if j == 6:
            plain(0)
            heard(1)
            tell(2)

    z = {}

    def own(k):
        y2[0, k].wait_recv()
        y2[1, k].wait_recv()
        mine[:, 0, k] = mine[:, 0, k] + Y2[0, k] + Y2[1, k]
        z[k] = send(mine.at[1, 0, k], ZR.at[k], z_s.at[k], z_r.at[k], across)

    def step(k, gradient):
        cols = slice(k * 128, k * 128 + 128)
        velocity = 0.5 * MO[:, cols] + gradient
        GR[:, cols] = gradient
        CUR[:, cols] = WT[:, cols] - LEARNING_RATE * velocity

    def transpose_out(k):
        cols = slice(k * 128, k * 128 + 128)
        for to in others:
            rows = pl.ds(pl.multiple_of(to * 8, 8), 8)
            send(CUR.at[rows, cols], RX.at[w, :, cols], a_s.at[k], a_r.at[k], {"worker": to, "tok": flip})

    def finish(k):
        z[k].wait_recv()
        step(k, mine[0, 0, k] + ZR[k])
        transpose_out(k)

    w1, w2 = {}, {}

    def across_one():
        for dy in (2, 1, 3, 0):
            zf[dy].wait_recv()
            mine[0, dy, 6:8] = mine[0, dy, 6:8] + ZF[dy]
        for k in range(2):
            w1[k] = send(mine.at[0, 2, 6 + k], W1.at[k], w1_s.at[k], w1_r.at[k], (up, down)[k])

    def across_two(k):
        dy = (1, 3)[k]
        w1[k].wait_recv()
        mine[0, dy, 6 + k] = mine[0, dy, 6 + k] + W1[k]
        for side in range(2):
            w2[side, k] = send(
                mine.at[0, (1, 3)[side], 6 + k], W2.at[side, k], w2_s.at[side, k], w2_r.at[side, k], (up, down)[side]
            )

    def finish_across(k):
        for side in range(2):
            w2[side, k].wait_recv()
        step(6 + k, mine[0, 0, 6 + k] + W2[0, k] + W2[1, k])
        transpose_out(6 + k)

    joined(0)
    joined(1)
    add_sibling(7)
    heard(2)
    tell(3)
    joined(2)
    plain(2)
    plain(3)
    joined(3)
    w_load.wait()
    m_load.wait()
    heard(3)
    for peer in work_peers:
        send(MS, MR.at[w], m_s.at[0], m_r.at[0], peer)
    own(0)
    own(1)
    across_one()
    joined(4)
    plain(4)
    plain(5)
    joined(5)
    finish(0)
    finish(1)
    own(2)
    own(3)
    across_two(0)
    across_two(1)
    finish(2)
    finish(3)

    def distances(half):
        for bi in range(4):
            for bj in range(bi, 4):
                which = [(i, j) for i in range(4) for j in range(i + 1 if bi == bj else 0, 4)]

                def tiles(tile, acc, bi=bi, bj=bj, which=which):
                    cols = pl.ds(pl.multiple_of(half * 512 + tile * 128, 128), 128)
                    left = [RX[4 * bi + i, :, cols] for i in range(4)]
                    right = left if bi == bj else [RX[4 * bj + i, :, cols] for i in range(4)]
                    diffs = [left[i] - right[j] for i, j in which]
                    return tuple(a + e * e for a, e in zip(acc, diffs))

                acc = lax.fori_loop(0, 4, tiles, tuple(jnp.zeros((8, 128), F32) for _ in which))
                for (i, j), total in zip(which, acc):
                    row = jnp.sum(total, axis=0, keepdims=True)
                    for a, b in ((4 * bi + i, 4 * bj + j), (4 * bj + j, 4 * bi + i)):
                        at = half * 256 + a * 16 + b
                        DP[at : at + 1, :] = row

    def wait_rows(half):
        for k in range(4 * half, 4 * half + 4):
            wait_bytes(RX.at[:, :, k * 128 : k * 128 + 128], a_r.at[k])

    own(4)
    own(5)
    finish(4)
    finish(5)
    finish_across(0)
    finish_across(1)
    put = pltpu.make_async_copy(GR, o_grad, g_s.at[0])
    put.start()
    wait_rows(0)
    distances(0)
    wait_bytes(MR.at[0:15], m_r.at[0])
    wait_rows(1)
    distances(1)

    packed = lax.dot_general(
        jnp.ones((8, 128), F32), DP[...], (((1,), (1,)), ((), ())), precision=HIGHEST, preferred_element_type=F32
    )
    PAY[0] = jnp.zeros((8, 128), F32)
    for r in range(4):
        PAY[0, r : r + 1, :] = packed[0:1, r * 128 : r * 128 + 128]
    for stage, (peers, got) in enumerate(((tok_peers, R1), (work_peers, R2))):
        for i, peer in enumerate(peers):
            send(PAY.at[stage, 0:4], got.at[i, 0:4], r_s.at[stage], r_r.at[stage], peer)
        total = PAY[stage, 0:4]
        wait_bytes(got.at[:, 0:4], r_r.at[stage])
        for i in range(15):
            total = total + got[i, 0:4]
        PAY[stage + 1, 0:4] = total

    row = lax.broadcasted_iota(jnp.int32, (32, 128), 0)
    lane = lax.broadcasted_iota(jnp.int32, (32, 128), 1)
    me = row & 15
    base = row - me
    masks = [
        (lane == base + other).astype(F32) for other in (me ^ 1, me ^ 2, (me + 12) & 15, (me + 4) & 15)
    ]
    eye = (lane == row).astype(F32)
    spread = jnp.concatenate([jnp.broadcast_to(PAY[2, r : r + 1, :], (8, 128)) for r in range(4)], axis=0)
    spread = jnp.where((lane >> 4) == (row & 7), spread, 0.0)
    from_lane = lax.broadcasted_iota(jnp.int32, (128, 128), 0)
    to_lane = lax.broadcasted_iota(jnp.int32, (128, 128), 1)
    pick = ((from_lane & 15) == (to_lane & 15)).astype(F32)
    dist2 = jnp.dot(spread, pick, precision=HIGHEST, preferred_element_type=F32)
    dist2 = jnp.where((lane >> 4) == (row >> 4), dist2, 0.0)
    pad = jnp.zeros((96, 128), F32)

    mixing = MR[:, 0, :]
    lane16 = lax.broadcasted_iota(jnp.int32, (16, 128), 1)
    shares = mixing / jnp.sum(mixing, axis=1, keepdims=True)
    share = []
    for k in range(4):
        one = jnp.sum(jnp.where(lane16 == k + 1, shares, 0.0), axis=1, keepdims=True)
        share.append(jnp.concatenate([one, one], axis=0))

    for round_index in range(ROUNDS):
        radius = clip[round_index].astype(F32) * (math.sqrt(D * KV_WIDTH) / 1000.0)
        moves = []
        for k in range(4):
            squares = jnp.sum(dist2 * masks[k], axis=1, keepdims=True)
            factor = radius / jnp.maximum(jnp.sqrt(jnp.maximum(squares, 0.0)), radius)
            moves.append(jnp.broadcast_to(share[k] * factor, (32, 128)))
            KC[round_index, k] = moves[k]
        if round_index == 0:
            mixer = eye * (1.0 - (moves[0] + moves[1] + moves[2] + moves[3]))
            for k in range(4):
                mixer = mixer + masks[k] * moves[k]
            left = jnp.dot(
                mixer, jnp.concatenate([dist2, pad], axis=0), precision=HIGHEST, preferred_element_type=F32
            )
            both = lax.dot_general(
                left, jnp.concatenate([mixer, pad], axis=0), (((1,), (1,)), ((), ())),
                precision=HIGHEST, preferred_element_type=F32,
            )
            diagonal = both * eye
            by_row = jnp.sum(diagonal, axis=1, keepdims=True)
            by_lane = jnp.sum(diagonal, axis=0, keepdims=True)
            dist2 = both - 0.5 * (by_row + by_lane)

    neighbours = [(i ^ 1, i ^ 2, (i - 4) % 16, (i + 4) % 16) for i in range(16)]

    def mixed(round_index, half, blocks):
        out = []
        for i in range(16):
            moved = None
            for k, j in enumerate(neighbours[i]):
                by = jnp.broadcast_to(KC[round_index, k, half * 16 + i : half * 16 + i + 1, :], (8, 128))
                term = by * (blocks[j] - blocks[i])
                moved = term if moved is None else moved + term
            out.append(moved)
        return out

    here = pl.ds(pl.multiple_of(w * 8, 8), 8)
    for half in range(2):

        def columns(tile, _, half=half):
            cols = pl.ds(pl.multiple_of(half * 512 + tile * 128, 128), 128)
            blocks = [RX[i, :, cols] for i in range(16)]
            first = mixed(0, half, blocks)
            second = mixed(1, half, [b + m for b, m in zip(blocks, first)])
            for i in range(16):
                NEW[i, :, cols] = first[i] + second[i]
            return 0

        lax.fori_loop(0, 4, columns, 0)
        cols = slice(half * 512, half * 512 + 512)
        for to in others:
            send(NEW.at[to, :, cols], o_move.at[here, cols], b_s.at[half], b_r.at[half], {"worker": to, "tok": flip})

    for cp in list(d.values()) + list(y1.values()) + list(y2.values()) + list(z.values()):
        cp.wait_send()
    for cp in list(zf.values()) + list(w1.values()) + list(w2.values()):
        cp.wait_send()
    wait_bytes(MR.at[0:15], m_s.at[0])
    for stage, got in enumerate((R1, R2)):
        wait_bytes(got.at[:, 0:4], r_s.at[stage])
    for k in range(8):
        wait_bytes(CUR.at[:, k * 128 : k * 128 + 128], a_s.at[k])
    put.wait()
    for half in range(2):
        cols = slice(half * 512, half * 512 + 512)
        wait_bytes(NEW.at[:, :, cols], b_s.at[half])
        wait_bytes(o_move.at[:, cols], b_r.at[half])


def per_device(inputs, cotangent, weights, momentum, mix_weights, clip_radius):
    vmem = pl.BlockSpec(memory_space=pltpu.VMEM)
    hbm = pl.BlockSpec(memory_space=pl.ANY)
    dma = pltpu.SemaphoreType.DMA
    block = jax.ShapeDtypeStruct((128, 1024), F32)
    moved, gradient = pl.pallas_call(
        kernel,
        out_shape=(block, block),
        in_specs=[hbm, hbm, hbm, hbm, vmem, pl.BlockSpec(memory_space=pltpu.SMEM)],
        out_specs=(hbm, hbm),
        scratch_shapes=[
            pltpu.VMEM((8, 1536, 256), BF16),
            pltpu.VMEM((4, 1536, 256), BF16),
            pltpu.VMEM((2, 2, 4, 8, 128, 128), F32),
            pltpu.VMEM((2, 4, 8, 128, 128), F32),
            pltpu.VMEM((6, 2, 128, 128), F32),
            pltpu.VMEM((2, 6, 2, 128, 128), F32),
            pltpu.VMEM((6, 128, 128), F32),
            pltpu.VMEM((4, 2, 128, 128), F32),
            pltpu.VMEM((2, 128, 128), F32),
            pltpu.VMEM((2, 2, 128, 128), F32),
            pltpu.VMEM((128, 1024), F32),
            pltpu.VMEM((128, 1024), F32),
            pltpu.VMEM((128, 1024), F32),
            pltpu.VMEM((128, 1024), F32),
            pltpu.VMEM((16, 8, 1024), F32),
            pltpu.VMEM((16, 8, 1024), F32),
            pltpu.VMEM((512, 128), F32),
            pltpu.VMEM((3, 8, 128), F32),
            pltpu.VMEM((15, 8, 128), F32),
            pltpu.VMEM((15, 8, 128), F32),
            pltpu.VMEM((8, 128), F32),
            pltpu.VMEM((16, 8, 128), F32),
            pltpu.VMEM((2, 4, 32, 128), F32),
            dma((14,)),
            dma((10,)), dma((10,)),
            dma((6,)), dma((6,)),
            dma((2, 6)), dma((2, 6)),
            dma((6,)), dma((6,)),
            dma((4,)), dma((4,)),
            dma((2,)), dma((2,)),
            dma((2, 2)), dma((2, 2)),
            dma((8,)), dma((8,)),
            dma((1,)), dma((1,)),
            dma((2,)), dma((2,)),
            dma((2,)), dma((2,)),
            dma((1,)),
            pltpu.SemaphoreType.REGULAR((4,)),
        ],
        compiler_params=pltpu.CompilerParams(
            collective_id=0, has_side_effects=True, vmem_limit_bytes=56 * 1024 * 1024
        ),
    )(inputs[0], cotangent[0], weights[0], momentum[0], mix_weights, clip_radius)
    velocity = 0.5 * momentum[0] + gradient
    new = (weights[0] - LEARNING_RATE * velocity) + moved
    return (new[None], velocity[None])


def solution(mesh):
    placed = (
        P("worker", "tok", None),
        P("worker", "tok", None),
        P("worker", "tok", None),
        P("worker", "tok", None),
        P("worker", None),
        P(),
    )
    return jax.shard_map(
        per_device,
        mesh=mesh,
        in_specs=placed,
        out_specs=(P("worker", "tok", None), P("worker", "tok", None)),
        check_vma=False,
    )
```

time: 93.1 us -> 82.2 us (0.88); the launches traced: 91.3 us -> 81.9 us
  Pallas kernels: 86.9 us -> 78.8 us
  local copies, waits for them, and re-layouts: 3.77 us -> 0.01 us
  other arithmetic: 0 us -> 2.39 us
    pallas_call x1, Pallas kernels: 86.9 us -> 78.8 us  [per_device(): pl.pallas_call(kernel, out_shape=(block, block), in_specs=[hbm, hbm, hbm,...]
    unnamed x2 -> x4, local copies, waits for them, and re-layouts: 3.77 us -> 0.01 us
    broadcast_in_dim x0 -> x1, other arithmetic: none -> 2.39 us  [per_device(): return (new[None], velocity[None])]
where the time goes in v2:
time: 82.2 us; the launch traced here: 81.9 us
  Pallas kernels  78.8 us (96%)
  other arithmetic  2.39 us (3%)
    pallas_call x1, Pallas kernels, per_device(): pl.pallas_call(kernel, out_shape=(block, block), in_specs=[hbm, hbm, hbm,...  78.8 us
    broadcast_in_dim x1, other arithmetic, per_device(): return (new[None], velocity[None])  2.39 us

profile of v2, /device:TPU:8, one launch (start us, length us, event | category | flops | bytes accessed | tf_op | source)
XLA Modules:
  0.0 81.9 jit_solution(5420473910293878634)
XLA Ops:
  0.6 0.0 copy-start.1
  0.6 0.0 copy-start
  0.7 78.8 %shard_map.77 = (f32[128,1024]{1,0:T(8,128)}, f32[128,1024]{1,0:T(8,128)}) custom-call(bf16[1536,2048]{1,0:T(8,128)(2,1)} %bitcast.11, bf16[1536,1024]{1,0:T(8,128)(2,1)} %bitcast.12, f32[128,1024]{1,0:T(8,128)} %bitcast.13, f32[128,1024]{1,0:T(8,128)} %bitcast.14, s32[1,5]{1,0:T(1,128)} %mix.1, s32[2]{0:T(128)} %clip.1), custom_call_target="tpu_custom_call" | custom-call | tf_op jit(solution)/shard_map/pallas_call | solution.py:422
  79.5 0.0 copy-done.1
  79.5 0.0 copy-done
  79.5 2.4 %fusion = (f32[1,128,1024]{2,1,0:T(8,128)}, f32[1,128,1024]{2,1,0:T(8,128)}) fusion(f32[128,1024]{1,0:T(8,128)} %get-tuple-element.4, f32[1,128,1024]{2,1,0:T(8,128)S(1)} %copy-done.1, f32[128,1024]{1,0:T(8,128)} %get-tuple-element.5, f32[1,128,1024]{2,1,0:T(8,128)S(1)} %copy-done), kind=kLoop, calls=%fused_computation.2 | loop fusion | flops 655360 | bytes 3145728 | tf_op jit(solution)/shard_map/broadcast_in_dim | solution.py:472
Async XLA Ops:
  0.6 78.9 %copy-start.1 = (f32[1,128,1024]{2,1,0:T(8,128)S(1)}, f32[1,128,1024]{2,1,0:T(8,128)}, u32[]{:S(2)}) copy-start(f32[1,128,1024]{2,1,0:T(8,128)} %param.9) | copy-start | bytes 1572868
  0.6 78.9 %copy-start = (f32[1,128,1024]{2,1,0:T(8,128)S(1)}, f32[1,128,1024]{2,1,0:T(8,128)}, u32[]{:S(2)}) copy-start(f32[1,128,1024]{2,1,0:T(8,128)} %param.8) | copy-start | bytes 1572868

commit v3 on v2

--- a/solution.py
+++ b/solution.py
@@ -29,39 +29,57 @@
 ):
     t = lax.axis_index("tok")
     w = lax.axis_index("worker")
-    q, y, c = t // 8, (t // 2) % 4, t % 2
-    flip = (1 - q) * 8 + y * 2 + c
-    sibling = {"worker": w, "tok": q * 8 + y * 2 + (1 - c)}
-    up = {"worker": w, "tok": q * 8 + lax.rem(y + 1, 4) * 2 + c}
-    down = {"worker": w, "tok": q * 8 + lax.rem(y + 3, 4) * 2 + c}
-    across = {"worker": w, "tok": flip}
-    h, x = w // 4, w % 4
-    tok_peers = [
-        {"worker": w, "tok": (q + dq) % 2 * 8 + lax.rem(y + dy, 4) * 2 + (c + dc) % 2}
-        for dy in (2, 1, 3, 0) for dq in (1, 0) for dc in (1, 0)
-    ][:-1]
-    others = [lax.rem(h + dh, 4) * 4 + lax.rem(x + dx, 4) for dx in (2, 1, 3, 0) for dh in (2, 1, 3, 0)]
-    work_peers = [{"worker": other, "tok": flip} for other in others[:-1]]
-    beyond = lax.rem(h + 2 * q + 3, 4)
-    next_to = [sibling, up, down, across] + [
-        {"worker": h * 4 + lax.rem(x + 1, 4), "tok": t},
-        {"worker": h * 4 + lax.rem(x + 3, 4), "tok": t},
-        {"worker": beyond * 4 + x, "tok": flip},
-    ]
-
-    def tell(n):
-        for peer in next_to:
-            pl.semaphore_signal(far.at[n], inc=1, device_id=peer, device_id_type=MESH)
-
-    def heard(n):
-        pl.semaphore_wait(far.at[n], 7)
-
-    barrier = pltpu.get_barrier_semaphore()
+    q, y, c = lax.div(t, 8), lax.rem(lax.div(t, 2), 4), lax.rem(t, 2)
 
     def load(src, dst, i):
         cp = pltpu.make_async_copy(src, dst, ld.at[i])
         cp.start()
         return cp
+
+    def feat_block(j):
+        dq, dy = ORDER[j]
+        chip = (1 - q if dq else q) * 4 + lax.rem(y + dy, 4)
+        return feat.at[:, pl.ds(pl.multiple_of(chip * 256, 256), 256)]
+
+    def load_feat(j):
+        f_loads[j] = load(feat_block(j), F.at[j], j)
+
+    def load_cot(n):
+        c_loads[n] = load(cot.at[:, n * 256 : (n + 1) * 256], C.at[n], 8 + n)
+
+    f_loads, c_loads = {}, {}
+    load_feat(0)
+    load_cot(0)
+    load_feat(1)
+
+    def chip_at(z, y, c):
+        return z * 8 + y * 2 + c
+
+    h, x = lax.div(w, 4), lax.rem(w, 4)
+    ys = [y] + [lax.rem(y + i, 4) for i in range(1, 4)]
+    hs = [h] + [lax.rem(h + i, 4) for i in range(1, 4)]
+    xs = [x] + [lax.rem(x + i, 4) for i in range(1, 4)]
+    flip = chip_at(1 - q, y, c)
+    sibling = {"worker": w, "tok": chip_at(q, y, 1 - c)}
+    up = {"worker": w, "tok": chip_at(q, ys[1], c)}
+    down = {"worker": w, "tok": chip_at(q, ys[3], c)}
+    across = {"worker": w, "tok": flip}
+    beyond = lax.rem(h + 2 * q + 3, 4)
+    next_to = [sibling, up, down, across] + [
+        {"worker": h * 4 + xs[1], "tok": t},
+        {"worker": h * 4 + xs[3], "tok": t},
+        {"worker": beyond * 4 + x, "tok": flip},
+    ]
+    barrier = pltpu.get_barrier_semaphore()
+    for peer in next_to:
+        pl.semaphore_signal(barrier, inc=1, device_id=peer, device_id_type=MESH)
+
+    def tell(n):
+        for peer in next_to:
+            pl.semaphore_signal(far.at[n], inc=1, device_id=peer, device_id_type=MESH)
+
+    def heard(n):
+        pl.semaphore_wait(far.at[n], 7)
 
     def send(src, dst, ss, rs, peer):
         cp = pltpu.make_async_remote_copy(
@@ -72,31 +90,6 @@
 
     def wait_bytes(ref, sem):
         pltpu.make_async_copy(ref, ref, sem).wait()
-
-    def feat_block(j):
-        dq, dy = ORDER[j]
-        chip = (q + dq) % 2 * 4 + lax.rem(y + dy, 4)
-        return feat.at[:, pl.ds(pl.multiple_of(chip * 256, 256), 256)]
-
-    def load_feat(j):
-        f_loads[j] = load(feat_block(j), F.at[j], j)
-
-    def load_cot(n):
-        c_loads[n] = load(cot.at[:, n * 256 : (n + 1) * 256], C.at[n], 8 + n)
-
-    f_loads, c_loads = {}, {}
-    load_feat(0)
-    load_cot(0)
-    load_feat(1)
-    for peer in next_to:
-        pl.semaphore_signal(barrier, inc=1, device_id=peer, device_id_type=MESH)
-
-    MS[...] = jnp.zeros_like(MS)
-    MS[0:1, 0:5] = mix[...].astype(F32)
-    MR[w] = MS[...]
-    for half in range(2):
-        for i in range(16):
-            DP[half * 256 + i * 17 : half * 256 + i * 17 + 1, :] = jnp.zeros((1, 128), F32)
 
     mine = PA.at[c]
 
@@ -125,12 +118,13 @@
 
     for n in range(4):
         for j in range(2):
+            if n == 0 and j == 0:
+                load_cot(1)
             if n == 0:
                 f_loads[j].wait()
             if j == 0:
                 c_loads[n].wait()
             if n == 0 and j == 0:
-                load_cot(1)
                 load_cot(2)
             product(j, n)
         if n == 0:
@@ -146,6 +140,12 @@
             opposite(n - 1)
     w_load, m_load = load(wts, WT, 12), load(mom, MO, 13)
     tell(0)
+    tok_peers = [
+        {"worker": w, "tok": chip_at(z_at, ys[dy], core)}
+        for dy in (2, 1, 3, 0) for z_at in (1 - q, q) for core in (1 - c, c)
+    ][:-1]
+    others = [hs[dh] * 4 + xs[dx] for dx in (2, 1, 3, 0) for dh in (2, 1, 3, 0)]
+    work_peers = [{"worker": other, "tok": flip} for other in others[:-1]]
 
     def add_sibling(j):
         dq, dy = ORDER[j]
@@ -248,6 +248,12 @@
     joined(3)
     w_load.wait()
     m_load.wait()
+    MS[...] = jnp.zeros_like(MS)
+    MS[0:1, 0:5] = mix[...].astype(F32)
+    MR[w] = MS[...]
+    for half in range(2):
+        for i in range(16):
+            DP[half * 256 + i * 17 : half * 256 + i * 17 + 1, :] = jnp.zeros((1, 128), F32)
     heard(3)
     for peer in work_peers:
         send(MS, MR.at[w], m_s.at[0], m_r.at[0], peer)
@@ -290,83 +296,69 @@
         for k in range(4 * half, 4 * half + 4):
             wait_bytes(RX.at[:, :, k * 128 : k * 128 + 128], a_r.at[k])
 
-    own(4)
-    own(5)
-    finish(4)
-    finish(5)
-    finish_across(0)
-    finish_across(1)
-    put = pltpu.make_async_copy(GR, o_grad, g_s.at[0])
-    put.start()
-    wait_rows(0)
-    distances(0)
-    wait_bytes(MR.at[0:15], m_r.at[0])
-    wait_rows(1)
-    distances(1)
-
-    packed = lax.dot_general(
-        jnp.ones((8, 128), F32), DP[...], (((1,), (1,)), ((), ())), precision=HIGHEST, preferred_element_type=F32
-    )
-    PAY[0] = jnp.zeros((8, 128), F32)
-    for r in range(4):
-        PAY[0, r : r + 1, :] = packed[0:1, r * 128 : r * 128 + 128]
-    for stage, (peers, got) in enumerate(((tok_peers, R1), (work_peers, R2))):
+    def pack(half):
+        packed = lax.dot_general(
+            jnp.ones((8, 128), F32), DP[half * 256 : half * 256 + 256, :], (((1,), (1,)), ((), ())),
+            precision=HIGHEST, preferred_element_type=F32,
+        )
+        for r in range(2):
+            PAY[half, 0, r : r + 1, :] = packed[0:1, r * 128 : r * 128 + 128]
+
+    stages = ((tok_peers, R1), (work_peers, R2))
+
+    def share_out(half, stage):
+        peers, got = stages[stage]
         for i, peer in enumerate(peers):
-            send(PAY.at[stage, 0:4], got.at[i, 0:4], r_s.at[stage], r_r.at[stage], peer)
-        total = PAY[stage, 0:4]
-        wait_bytes(got.at[:, 0:4], r_r.at[stage])
-        for i in range(15):
-            total = total + got[i, 0:4]
-        PAY[stage + 1, 0:4] = total
-
-    row = lax.broadcasted_iota(jnp.int32, (32, 128), 0)
-    lane = lax.broadcasted_iota(jnp.int32, (32, 128), 1)
-    me = row & 15
-    base = row - me
-    masks = [
-        (lane == base + other).astype(F32) for other in (me ^ 1, me ^ 2, (me + 12) & 15, (me + 4) & 15)
-    ]
-    eye = (lane == row).astype(F32)
-    spread = jnp.concatenate([jnp.broadcast_to(PAY[2, r : r + 1, :], (8, 128)) for r in range(4)], axis=0)
-    spread = jnp.where((lane >> 4) == (row & 7), spread, 0.0)
-    from_lane = lax.broadcasted_iota(jnp.int32, (128, 128), 0)
-    to_lane = lax.broadcasted_iota(jnp.int32, (128, 128), 1)
-    pick = ((from_lane & 15) == (to_lane & 15)).astype(F32)
-    dist2 = jnp.dot(spread, pick, precision=HIGHEST, preferred_element_type=F32)
-    dist2 = jnp.where((lane >> 4) == (row >> 4), dist2, 0.0)
-    pad = jnp.zeros((96, 128), F32)
-
-    mixing = MR[:, 0, :]
-    lane16 = lax.broadcasted_iota(jnp.int32, (16, 128), 1)
-    shares = mixing / jnp.sum(mixing, axis=1, keepdims=True)
-    share = []
-    for k in range(4):
-        one = jnp.sum(jnp.where(lane16 == k + 1, shares, 0.0), axis=1, keepdims=True)
-        share.append(jnp.concatenate([one, one], axis=0))
-
-    for round_index in range(ROUNDS):
-        radius = clip[round_index].astype(F32) * (math.sqrt(D * KV_WIDTH) / 1000.0)
-        moves = []
-        for k in range(4):
-            squares = jnp.sum(dist2 * masks[k], axis=1, keepdims=True)
-            factor = radius / jnp.maximum(jnp.sqrt(jnp.maximum(squares, 0.0)), radius)
-            moves.append(jnp.broadcast_to(share[k] * factor, (32, 128)))
-            KC[round_index, k] = moves[k]
-        if round_index == 0:
-            mixer = eye * (1.0 - (moves[0] + moves[1] + moves[2] + moves[3]))
+            send(PAY.at[half, stage, 0:2], got.at[half, i, 0:2], r_s.at[half, stage], r_r.at[half, stage], peer)
+
+    def add_up(half, stage):
+        got = stages[stage][1]
+        wait_bytes(got.at[half, :, 0:2], r_r.at[half, stage])
+        parts = [PAY[half, stage, 0:2]] + [got[half, i, 0:2] for i in range(15)]
+        while len(parts) > 1:
+            parts = [a + b for a, b in zip(parts[::2], parts[1::2])]
+        PAY[half, stage + 1, 0:2] = parts[0]
+
+    def constants():
+        row = lax.broadcasted_iota(jnp.int32, (16, 128), 0)
+        lane = lax.broadcasted_iota(jnp.int32, (16, 128), 1)
+        masks = [(lane == other).astype(F32) for other in (row ^ 1, row ^ 2, (row + 12) & 15, (row + 4) & 15)]
+        from_lane = lax.broadcasted_iota(jnp.int32, (128, 128), 0)
+        to_lane = lax.broadcasted_iota(jnp.int32, (128, 128), 1)
+        pick = ((from_lane & 15) == to_lane).astype(F32)
+        mixing = MR[:, 0, :]
+        shares = mixing / jnp.sum(mixing, axis=1, keepdims=True)
+        share = [jnp.sum(jnp.where(lane == k + 1, shares, 0.0), axis=1, keepdims=True) for k in range(4)]
+        return (lane >> 4) == (row & 7), masks, (lane == row).astype(F32), pick, share
+
+    def solve(half):
+        place, masks, eye, pick, share = constants()
+        spread = jnp.concatenate([jnp.broadcast_to(PAY[half, 2, r : r + 1, :], (8, 128)) for r in range(2)], axis=0)
+        dist2 = jnp.dot(jnp.where(place, spread, 0.0), pick, precision=HIGHEST, preferred_element_type=F32)
+        pad = jnp.zeros((112, 128), F32)
+        for round_index in range(ROUNDS):
+            radius = clip[round_index].astype(F32) * (math.sqrt(D * KV_WIDTH) / 1000.0)
+            moves = []
             for k in range(4):
-                mixer = mixer + masks[k] * moves[k]
-            left = jnp.dot(
-                mixer, jnp.concatenate([dist2, pad], axis=0), precision=HIGHEST, preferred_element_type=F32
-            )
-            both = lax.dot_general(
-                left, jnp.concatenate([mixer, pad], axis=0), (((1,), (1,)), ((), ())),
-                precision=HIGHEST, preferred_element_type=F32,
-            )
-            diagonal = both * eye
-            by_row = jnp.sum(diagonal, axis=1, keepdims=True)
-            by_lane = jnp.sum(diagonal, axis=0, keepdims=True)
-            dist2 = both - 0.5 * (by_row + by_lane)
+                squares = jnp.sum(dist2 * masks[k], axis=1, keepdims=True)
+                factor = radius / jnp.maximum(jnp.sqrt(jnp.maximum(squares, 0.0)), radius)
+                moves.append(jnp.broadcast_to(share[k] * factor, (16, 128)))
+                KC[round_index, k, half * 16 : half * 16 + 16, :] = moves[k]
+            if round_index == 0:
+                mixer = eye * (1.0 - (moves[0] + moves[1] + moves[2] + moves[3]))
+                for k in range(4):
+                    mixer = mixer + masks[k] * moves[k]
+                left = jnp.dot(
+                    mixer, jnp.concatenate([dist2, pad], axis=0), precision=HIGHEST, preferred_element_type=F32
+                )
+                both = lax.dot_general(
+                    left, jnp.concatenate([mixer, pad], axis=0), (((1,), (1,)), ((), ())),
+                    precision=HIGHEST, preferred_element_type=F32,
+                )
+                diagonal = both * eye
+                by_row = jnp.sum(diagonal, axis=1, keepdims=True)
+                by_lane = jnp.sum(diagonal, axis=0, keepdims=True)
+                dist2 = both - 0.5 * (by_row + by_lane)
 
     neighbours = [(i ^ 1, i ^ 2, (i - 4) % 16, (i + 4) % 16) for i in range(16)]
 
@@ -382,9 +374,11 @@
         return out
 
     here = pl.ds(pl.multiple_of(w * 8, 8), 8)
-    for half in range(2):
-
-        def columns(tile, _, half=half):
+
+    def gossip(half):
+        solve(half)
+
+        def columns(tile, _):
             cols = pl.ds(pl.multiple_of(half * 512 + tile * 128, 128), 128)
             blocks = [RX[i, :, cols] for i in range(16)]
             first = mixed(0, half, blocks)
@@ -398,13 +392,40 @@
         for to in others:
             send(NEW.at[to, :, cols], o_move.at[here, cols], b_s.at[half], b_r.at[half], {"worker": to, "tok": flip})
 
+    own(4)
+    own(5)
+    wait_rows(0)
+    distances(0)
+    pack(0)
+    share_out(0, 0)
+    finish(4)
+    finish(5)
+    finish_across(0)
+    finish_across(1)
+    put = pltpu.make_async_copy(GR, o_grad, g_s.at[0])
+    put.start()
+    add_up(0, 0)
+    share_out(0, 1)
+    wait_bytes(MR.at[0:15], m_r.at[0])
+    wait_rows(1)
+    distances(1)
+    pack(1)
+    share_out(1, 0)
+    add_up(0, 1)
+    gossip(0)
+    add_up(1, 0)
+    share_out(1, 1)
+    add_up(1, 1)
+    gossip(1)
+
     for cp in list(d.values()) + list(y1.values()) + list(y2.values()) + list(z.values()):
         cp.wait_send()
     for cp in list(zf.values()) + list(w1.values()) + list(w2.values()):
         cp.wait_send()
     wait_bytes(MR.at[0:15], m_s.at[0])
-    for stage, got in enumerate((R1, R2)):
-        wait_bytes(got.at[:, 0:4], r_s.at[stage])
+    for half in range(2):
+        for stage, got in enumerate((R1, R2)):
+            wait_bytes(got.at[half, :, 0:2], r_s.at[half, stage])
     for k in range(8):
         wait_bytes(CUR.at[:, k * 128 : k * 128 + 128], a_s.at[k])
     put.wait()
@@ -442,9 +463,9 @@
             pltpu.VMEM((16, 8, 1024), F32),
             pltpu.VMEM((16, 8, 1024), F32),
             pltpu.VMEM((512, 128), F32),
-            pltpu.VMEM((3, 8, 128), F32),
-            pltpu.VMEM((15, 8, 128), F32),
-            pltpu.VMEM((15, 8, 128), F32),
+            pltpu.VMEM((2, 3, 8, 128), F32),
+            pltpu.VMEM((2, 15, 8, 128), F32),
+            pltpu.VMEM((2, 15, 8, 128), F32),
             pltpu.VMEM((8, 128), F32),
             pltpu.VMEM((16, 8, 128), F32),
             pltpu.VMEM((2, 4, 32, 128), F32),
@@ -458,7 +479,7 @@
             dma((2, 2)), dma((2, 2)),
             dma((8,)), dma((8,)),
             dma((1,)), dma((1,)),
-            dma((2,)), dma((2,)),
+            dma((2, 2)), dma((2, 2)),
             dma((2,)), dma((2,)),
             dma((1,)),
             pltpu.SemaphoreType.REGULAR((4,)),

time: 82.2 us -> 78.2 us (0.951)
  Pallas kernels: 78.8 us -> 74.7 us
    pallas_call x1, Pallas kernels: 78.8 us -> 74.7 us  [per_device(): pl.pallas_call(kernel, out_shape=(block, block), in_specs=[hbm, hbm, hbm,...]
where the time goes in v3:
time: 78.2 us; the launch traced here: 77.7 us
  Pallas kernels  74.7 us (96%)
  other arithmetic  2.39 us (3%)
    pallas_call x1, Pallas kernels, per_device(): pl.pallas_call(kernel, out_shape=(block, block), in_specs=[hbm, hbm, hbm,...  74.7 us
    broadcast_in_dim x1, other arithmetic, per_device(): return (new[None], velocity[None])  2.39 us

profile of v3, /device:TPU:8, one launch (start us, length us, event | category | flops | bytes accessed | tf_op | source)
XLA Modules:
  0.0 77.7 jit_solution(6185416538892425146)
XLA Ops:
  0.6 0.0 copy-start.1
  0.6 0.0 copy-start
  0.7 74.7 %shard_map.77 = (f32[128,1024]{1,0:T(8,128)}, f32[128,1024]{1,0:T(8,128)}) custom-call(bf16[1536,2048]{1,0:T(8,128)(2,1)} %bitcast.11, bf16[1536,1024]{1,0:T(8,128)(2,1)} %bitcast.12, f32[128,1024]{1,0:T(8,128)} %bitcast.13, f32[128,1024]{1,0:T(8,128)} %bitcast.14, s32[1,5]{1,0:T(1,128)} %mix.1, s32[2]{0:T(128)} %clip.1), custom_call_target="tpu_custom_call" | custom-call | tf_op jit(solution)/shard_map/pallas_call | solution.py:443
  75.3 0.0 copy-done.1
  75.3 0.0 copy-done
  75.3 2.4 %fusion = (f32[1,128,1024]{2,1,0:T(8,128)}, f32[1,128,1024]{2,1,0:T(8,128)}) fusion(f32[128,1024]{1,0:T(8,128)} %get-tuple-element.4, f32[1,128,1024]{2,1,0:T(8,128)S(1)} %copy-done.1, f32[128,1024]{1,0:T(8,128)} %get-tuple-element.5, f32[1,128,1024]{2,1,0:T(8,128)S(1)} %copy-done), kind=kLoop, calls=%fused_computation.2 | loop fusion | flops 655360 | bytes 3145728 | tf_op jit(solution)/shard_map/broadcast_in_dim | solution.py:493
Async XLA Ops:
  0.6 74.7 %copy-start.1 = (f32[1,128,1024]{2,1,0:T(8,128)S(1)}, f32[1,128,1024]{2,1,0:T(8,128)}, u32[]{:S(2)}) copy-start(f32[1,128,1024]{2,1,0:T(8,128)} %param.9) | copy-start | bytes 1572868
  0.6 74.7 %copy-start = (f32[1,128,1024]{2,1,0:T(8,128)S(1)}, f32[1,128,1024]{2,1,0:T(8,128)}, u32[]{:S(2)}) copy-start(f32[1,128,1024]{2,1,0:T(8,128)} %param.8) | copy-start | bytes 1572868

commit v4 on v3

--- a/solution.py
+++ b/solution.py
@@ -23,7 +23,7 @@
 
 def kernel(
     feat, cot, wts, mom, mix, clip, o_move, o_grad,
-    F, C, PA, PR, Y1, Y2, ZR, ZF, W1, W2, WT, MO, CUR, GR, RX, NEW, DP, PAY, R1, R2, MS, MR, KC,
+    F, C, PA, PR, Y1, Y2, ZR, ZF, W1, W2, WT, MO, CUR, GR, RX, NEW, DP, PAY, R1, R2, MS, MR, SH, KC,
     ld, d_s, d_r, y1_s, y1_r, y2_s, y2_r, z_s, z_r, zf_s, zf_r, w1_s, w1_r, w2_s, w2_r,
     a_s, a_r, m_s, m_r, r_s, r_r, b_s, b_r, g_s, far,
 ):
@@ -202,16 +202,26 @@
         GR[:, cols] = gradient
         CUR[:, cols] = WT[:, cols] - LEARNING_RATE * velocity
 
-    def transpose_out(k):
-        cols = slice(k * 128, k * 128 + 128)
+    groups = ((0,), (1,), (2,), (3,), (4,), (5,), (6, 7))
+
+    def columns_of(group):
+        return slice(group[0] * 128, group[-1] * 128 + 128)
+
+    def transpose_out(group):
+        k, cols = group[0], columns_of(group)
         for to in others:
             rows = pl.ds(pl.multiple_of(to * 8, 8), 8)
             send(CUR.at[rows, cols], RX.at[w, :, cols], a_s.at[k], a_r.at[k], {"worker": to, "tok": flip})
 
+    def leave(k):
+        for group in groups:
+            if group[-1] == k:
+                transpose_out(group)
+
     def finish(k):
         z[k].wait_recv()
         step(k, mine[0, 0, k] + ZR[k])
-        transpose_out(k)
+        leave(k)
 
     w1, w2 = {}, {}
 
@@ -235,7 +245,7 @@
         for side in range(2):
             w2[side, k].wait_recv()
         step(6 + k, mine[0, 0, 6 + k] + W2[0, k] + W2[1, k])
-        transpose_out(6 + k)
+        leave(6 + k)
 
     joined(0)
     joined(1)
@@ -257,9 +267,9 @@
     heard(3)
     for peer in work_peers:
         send(MS, MR.at[w], m_s.at[0], m_r.at[0], peer)
+    across_one()
     own(0)
     own(1)
-    across_one()
     joined(4)
     plain(4)
     plain(5)
@@ -293,8 +303,9 @@
                         DP[at : at + 1, :] = row
 
     def wait_rows(half):
-        for k in range(4 * half, 4 * half + 4):
-            wait_bytes(RX.at[:, :, k * 128 : k * 128 + 128], a_r.at[k])
+        for group in groups:
+            if group[0] // 4 == half:
+                wait_bytes(RX.at[:, :, columns_of(group)], a_r.at[group[0]])
 
     def pack(half):
         packed = lax.dot_general(
@@ -326,13 +337,18 @@
         from_lane = lax.broadcasted_iota(jnp.int32, (128, 128), 0)
         to_lane = lax.broadcasted_iota(jnp.int32, (128, 128), 1)
         pick = ((from_lane & 15) == to_lane).astype(F32)
+        return (lane >> 4) == (row & 7), masks, (lane == row).astype(F32), pick
+
+    def take_shares():
+        lane = lax.broadcasted_iota(jnp.int32, (16, 128), 1)
         mixing = MR[:, 0, :]
         shares = mixing / jnp.sum(mixing, axis=1, keepdims=True)
-        share = [jnp.sum(jnp.where(lane == k + 1, shares, 0.0), axis=1, keepdims=True) for k in range(4)]
-        return (lane >> 4) == (row & 7), masks, (lane == row).astype(F32), pick, share
+        for k in range(4):
+            share = jnp.sum(jnp.where(lane == k + 1, shares, 0.0), axis=1, keepdims=True)
+            SH[k] = jnp.broadcast_to(share, (16, 128))
 
     def solve(half):
-        place, masks, eye, pick, share = constants()
+        place, masks, eye, pick = constants()
         spread = jnp.concatenate([jnp.broadcast_to(PAY[half, 2, r : r + 1, :], (8, 128)) for r in range(2)], axis=0)
         dist2 = jnp.dot(jnp.where(place, spread, 0.0), pick, precision=HIGHEST, preferred_element_type=F32)
         pad = jnp.zeros((112, 128), F32)
@@ -342,7 +358,7 @@
             for k in range(4):
                 squares = jnp.sum(dist2 * masks[k], axis=1, keepdims=True)
                 factor = radius / jnp.maximum(jnp.sqrt(jnp.maximum(squares, 0.0)), radius)
-                moves.append(jnp.broadcast_to(share[k] * factor, (16, 128)))
+                moves.append(SH[k] * factor)
                 KC[round_index, k, half * 16 : half * 16 + 16, :] = moves[k]
             if round_index == 0:
                 mixer = eye * (1.0 - (moves[0] + moves[1] + moves[2] + moves[3]))
@@ -375,8 +391,7 @@
 
     here = pl.ds(pl.multiple_of(w * 8, 8), 8)
 
-    def gossip(half):
-        solve(half)
+    def mix_rows(half):
 
         def columns(tile, _):
             cols = pl.ds(pl.multiple_of(half * 512 + tile * 128, 128), 128)
@@ -399,24 +414,27 @@
     pack(0)
     share_out(0, 0)
     finish(4)
+    finish_across(0)
     finish(5)
-    finish_across(0)
     finish_across(1)
     put = pltpu.make_async_copy(GR, o_grad, g_s.at[0])
     put.start()
     add_up(0, 0)
     share_out(0, 1)
     wait_bytes(MR.at[0:15], m_r.at[0])
+    take_shares()
     wait_rows(1)
     distances(1)
     pack(1)
     share_out(1, 0)
     add_up(0, 1)
-    gossip(0)
+    solve(0)
+    mix_rows(0)
     add_up(1, 0)
     share_out(1, 1)
     add_up(1, 1)
-    gossip(1)
+    solve(1)
+    mix_rows(1)
 
     for cp in list(d.values()) + list(y1.values()) + list(y2.values()) + list(z.values()):
         cp.wait_send()
@@ -426,8 +444,8 @@
     for half in range(2):
         for stage, got in enumerate((R1, R2)):
             wait_bytes(got.at[half, :, 0:2], r_s.at[half, stage])
-    for k in range(8):
-        wait_bytes(CUR.at[:, k * 128 : k * 128 + 128], a_s.at[k])
+    for group in groups:
+        wait_bytes(CUR.at[:, columns_of(group)], a_s.at[group[0]])
     put.wait()
     for half in range(2):
         cols = slice(half * 512, half * 512 + 512)
@@ -468,6 +486,7 @@
             pltpu.VMEM((2, 15, 8, 128), F32),
             pltpu.VMEM((8, 128), F32),
             pltpu.VMEM((16, 8, 128), F32),
+            pltpu.VMEM((4, 16, 128), F32),
             pltpu.VMEM((2, 4, 32, 128), F32),
             dma((14,)),
             dma((10,)), dma((10,)),

time: 78.2 us -> 77.7 us (level)
  no operation moved by 1% of the time
where the time goes in v4:
time: 77.7 us; the launch traced here: 77.6 us
  Pallas kernels  74.5 us (96%)
  other arithmetic  2.39 us (3%)
    pallas_call x1, Pallas kernels, per_device(): pl.pallas_call(kernel, out_shape=(block, block), in_specs=[hbm, hbm, hbm,...  74.5 us
    broadcast_in_dim x1, other arithmetic, per_device(): return (new[None], velocity[None])  2.39 us

profile of v4, /device:TPU:8, one launch (start us, length us, event | category | flops | bytes accessed | tf_op | source)
XLA Modules:
  0.0 77.6 jit_solution(10670949895537949425)
XLA Ops:
  0.6 0.0 copy-start.1
  0.6 0.0 copy-start
  0.7 74.5 %shard_map.77 = (f32[128,1024]{1,0:T(8,128)}, f32[128,1024]{1,0:T(8,128)}) custom-call(bf16[1536,2048]{1,0:T(8,128)(2,1)} %bitcast.11, bf16[1536,1024]{1,0:T(8,128)(2,1)} %bitcast.12, f32[128,1024]{1,0:T(8,128)} %bitcast.13, f32[128,1024]{1,0:T(8,128)} %bitcast.14, s32[1,5]{1,0:T(1,128)} %mix.1, s32[2]{0:T(128)} %clip.1), custom_call_target="tpu_custom_call" | custom-call | tf_op jit(solution)/shard_map/pallas_call | solution.py:461
  75.2 0.0 copy-done.1
  75.2 0.0 copy-done
  75.2 2.4 %fusion = (f32[1,128,1024]{2,1,0:T(8,128)}, f32[1,128,1024]{2,1,0:T(8,128)}) fusion(f32[128,1024]{1,0:T(8,128)} %get-tuple-element.4, f32[1,128,1024]{2,1,0:T(8,128)S(1)} %copy-done.1, f32[128,1024]{1,0:T(8,128)} %get-tuple-element.5, f32[1,128,1024]{2,1,0:T(8,128)S(1)} %copy-done), kind=kLoop, calls=%fused_computation.2 | loop fusion | flops 655360 | bytes 3145728 | tf_op jit(solution)/shard_map/broadcast_in_dim | solution.py:512
Async XLA Ops:
  0.6 74.6 %copy-start.1 = (f32[1,128,1024]{2,1,0:T(8,128)S(1)}, f32[1,128,1024]{2,1,0:T(8,128)}, u32[]{:S(2)}) copy-start(f32[1,128,1024]{2,1,0:T(8,128)} %param.9) | copy-start | bytes 1572868
  0.6 74.6 %copy-start = (f32[1,128,1024]{2,1,0:T(8,128)S(1)}, f32[1,128,1024]{2,1,0:T(8,128)}, u32[]{:S(2)}) copy-start(f32[1,128,1024]{2,1,0:T(8,128)} %param.8) | copy-start | bytes 1572868

commit v5 on v4

--- a/solution.py
+++ b/solution.py
@@ -126,15 +126,17 @@
                 c_loads[n].wait()
             if n == 0 and j == 0:
                 load_cot(2)
+                load_cot(3)
+                load_feat(2)
             product(j, n)
         if n == 0:
-            load_cot(3)
-            load_feat(2)
+            load_feat(3)
+            load_feat(4)
+            load_feat(5)
             pl.semaphore_wait(barrier, 7)
-        else:
-            load_feat(2 * n + 1)
-            if n < 3:
-                load_feat(2 * n + 2)
+        elif n == 1:
+            load_feat(6)
+            load_feat(7)
         d[n] = send(PA.at[1 - c, :, 2, 2 * n : 2 * n + 2], PR.at[:, 2, 2 * n : 2 * n + 2], d_s.at[n], d_r.at[n], sibling)
         if n >= 1:
             opposite(n - 1)

time: 77.7 us -> 77.8 us (level)
  no operation moved by 1% of the time
where the time goes in v5:
time: 77.8 us; the launch traced here: 77.7 us
  Pallas kernels  74.6 us (96%)
  other arithmetic  2.39 us (3%)
    pallas_call x1, Pallas kernels, per_device(): pl.pallas_call(kernel, out_shape=(block, block), in_specs=[hbm, hbm, hbm,...  74.6 us
    broadcast_in_dim x1, other arithmetic, per_device(): return (new[None], velocity[None])  2.39 us

profile of v5, /device:TPU:8, one launch (start us, length us, event | category | flops | bytes accessed | tf_op | source)
XLA Modules:
  0.0 77.7 jit_solution(10918009886092578392)
XLA Ops:
  0.6 0.0 copy-start.1
  0.6 0.0 copy-start
  0.7 74.6 %shard_map.77 = (f32[128,1024]{1,0:T(8,128)}, f32[128,1024]{1,0:T(8,128)}) custom-call(bf16[1536,2048]{1,0:T(8,128)(2,1)} %bitcast.11, bf16[1536,1024]{1,0:T(8,128)(2,1)} %bitcast.12, f32[128,1024]{1,0:T(8,128)} %bitcast.13, f32[128,1024]{1,0:T(8,128)} %bitcast.14, s32[1,5]{1,0:T(1,128)} %mix.1, s32[2]{0:T(128)} %clip.1), custom_call_target="tpu_custom_call" | custom-call | tf_op jit(solution)/shard_map/pallas_call | solution.py:463
  75.3 0.0 copy-done.1
  75.3 0.0 copy-done
  75.3 2.4 %fusion = (f32[1,128,1024]{2,1,0:T(8,128)}, f32[1,128,1024]{2,1,0:T(8,128)}) fusion(f32[128,1024]{1,0:T(8,128)} %get-tuple-element.4, f32[1,128,1024]{2,1,0:T(8,128)S(1)} %copy-done.1, f32[128,1024]{1,0:T(8,128)} %get-tuple-element.5, f32[1,128,1024]{2,1,0:T(8,128)S(1)} %copy-done), kind=kLoop, calls=%fused_computation.2 | loop fusion | flops 655360 | bytes 3145728 | tf_op jit(solution)/shard_map/broadcast_in_dim | solution.py:514
Async XLA Ops:
  0.6 74.7 %copy-start.1 = (f32[1,128,1024]{2,1,0:T(8,128)S(1)}, f32[1,128,1024]{2,1,0:T(8,128)}, u32[]{:S(2)}) copy-start(f32[1,128,1024]{2,1,0:T(8,128)} %param.9) | copy-start | bytes 1572868
  0.6 74.7 %copy-start = (f32[1,128,1024]{2,1,0:T(8,128)S(1)}, f32[1,128,1024]{2,1,0:T(8,128)}, u32[]{:S(2)}) copy-start(f32[1,128,1024]{2,1,0:T(8,128)} %param.8) | copy-start | bytes 1572868
